TPU v7x, 32 devices: a whole 2x2x4 slice. The times are simulated.
32 devices in a mesh: band: 4 (over x, core), gx: 4 (over z), gy: 2 (over y).
Axes of the slice: x: 2, y: 2, z: 4, core: 2. Of those that a mesh axis runs over, the one named last changes fastest.
Arguments:
- local_orbitals: float32 [4, 32, 32, 128], P('band', 'gx', 'gy'), may hold values from -14 to 14
- block_orbitals: float32 [24, 8, 32, 32, 128], P('band', None, 'gx', 'gy'), may hold values from -14 to 14
- occupation: float32 [24, 8], replicated, may hold values from 0.2 to 2
- owner: int32 [4], replicated, may hold values from 0 to 3
- block_id: int32 [4], replicated, may hold values from 0 to 5
Outputs:
- exchange: float32 [4, 32, 32, 128], P('band', 'gx', 'gy')
All inputs are finite; a program needn't handle non-finite values.
Results may differ from a plain program's by a relative error of at most 0.0001.
Values sent between devices are 32-bit elements; how exact they have to be, the bound alone decides.
A program may use at most 64 MiB of HBM per device.

v0:
```python
import jax
import jax.numpy as jnp
from jax import lax
from jax.sharding import PartitionSpec as P

ITERS = 4


SCREEN = 0.1


def padded_2(block, sides, width):
    for axis, dim in sides:
        count = lax.axis_size(axis)
        forward = [(i, i + 1) for i in range(count - 1)]
        forward.append((count - 1, 0))
        backward = [(target, source) for source, target in forward]
        low = lax.ppermute(
            lax.slice_in_dim(block, block.shape[dim] - width, None, axis=dim), axis, forward
        )
        high = lax.ppermute(lax.slice_in_dim(block, 0, width, axis=dim), axis, backward)
        block = jnp.concatenate([low, block, high], axis=dim)
    return block


def spread(value, axis, source):
    kept = jnp.where(lax.axis_index(axis) == source, value, 0).astype(value.dtype)
    return lax.psum(kept, axis)


def per_field(values):
    return values[:, None, None, None]


def neighbour_sum(padded):
    centre_cells = padded[:, 1:-1, 1:-1, :]
    beside = padded[:, 2:, 1:-1, :] + padded[:, :-2, 1:-1, :]
    beside = beside + padded[:, 1:-1, 2:, :] + padded[:, 1:-1, :-2, :]
    beside = beside + jnp.roll(centre_cells, 1, axis=3) + jnp.roll(centre_cells, -1, axis=3)
    return (6.0 + SCREEN) * centre_cells - beside


def apply_operator(field_in):
    padded = padded_2(field_in, (("gx", 1), ("gy", 2)), 1)
    return neighbour_sum(padded)


def partial_products(left, right):
    return jnp.sum(left * right, axis=(1, 2, 3))


def residual_sums(residual):
    return lax.psum(partial_products(residual, residual), ("gx", "gy"))


def solve_pairs(density):
    solution = jnp.zeros_like(density)
    residual = density
    direction = density
    norm_now = residual_sums(residual)
    for iteration in range(ITERS):
        image = apply_operator(direction)
        curvature = lax.psum(partial_products(direction, image), ("gx", "gy"))
        step_length = norm_now / curvature
        solution = solution + per_field(step_length) * direction
        if iteration + 1 < ITERS:
            residual = residual - per_field(step_length) * image
            norm_next = residual_sums(residual)
            direction = residual + per_field(norm_next / norm_now) * direction
            norm_now = norm_next
    return solution


def fetch_block(block_orbitals, occupation, owner, block_id, turn_index):
    owner_rank = owner[turn_index]
    local_pick = block_id[turn_index]
    chosen = lax.dynamic_index_in_dim(block_orbitals, local_pick, 0, keepdims=False)
    arrived = spread(chosen, "band", owner_rank)
    global_pick = owner_rank * block_orbitals.shape[0] + local_pick
    weights = lax.dynamic_index_in_dim(occupation, global_pick, 0, keepdims=False)
    return (arrived, weights)


def exchange_terms(local_ext, fields, weights):
    count_local = local_ext.shape[0]
    count_block = fields.shape[0]
    density = (local_ext[:, None] * fields[None]).reshape(
        (count_local * count_block,) + fields.shape[1:]
    )
    solution = solve_pairs(density)
    solution = solution.reshape((count_local, count_block) + fields.shape[1:])
    weighted = per_field(weights) * fields
    return jnp.sum(solution * weighted[None], axis=1)


def on_device(local_orbitals, block_orbitals, occupation, owner, block_id):
    result = jnp.zeros(local_orbitals.shape, jnp.float32)
    turn_count = owner.shape[0]
    for turn_index in range(turn_count):
        fields, weights = fetch_block(block_orbitals, occupation, owner, block_id, turn_index)
        result = result - exchange_terms(local_orbitals, fields, weights)
    return result


def solution(mesh):
    placed = (P("band", "gx", "gy", None), P("band", None, "gx", "gy", None), P(), P(), P())
    return jax.shard_map(
        on_device,
        mesh=mesh,
        in_specs=placed,
        out_specs=P("band", "gx", "gy", None),
        check_vma=False,
    )
```

profile of v0, /device:TPU:0, one launch (start us, length us, event | category | flops | bytes accessed | tf_op | source)
XLA Modules:
  0.0 618.0 jit_solution(4456818016891337228)
XLA Ops:
  19.3 2.9 select_bitcast_fusion.1
  28.0 49.1 %all-reduce.12.cloned.1.call-done = (f32[8,8,16,128]{3,2,1,0:T(8,128)}, f32[8,8,16,128]{3,2,1,0:T(8,128)}, f32[8,8,16,128]{3,2,1,0:T(8,128)}, f32[8,8,16,128]{3,2,1,0:T(8,128)}) async-done(((f32[8,8,16,128]{3,2,1,0:T(8,128)}, f32[8,8,16,128]{3,2,1,0:T(8,128)}, f32[8,8,16,128]{3,2,1,0:T(8,128)}, f32[8,8,16,128]{3,2,1,0:T(8,128)}), (f32[8,8,16,128]{3,2,1,0:T(8,128)}, f32[8,8,16,128]{3,2,1,0:T(8,128)}, ...) | async-done | bytes 2097168 | tf_op jit(solution)/shard_map/psum | solution.py:28
  81.6 3.3 collective-permute-start.16
  84.9 3.9 collective-permute-start
  88.8 3.8 collective-permute-start.32
  102.8 20.6 %all-reduce.8 = (f32[8]{0:T(128)S(1)}, f32[8]{0:T(128)S(1)}) all-reduce(f32[8]{0:T(128)S(1)} %get-tuple-element.6, f32[8]{0:T(128)S(1)} %get-tuple-element.5), channel_id=1, replica_groups=mesh['band'=4,'gx'=4,'gy'=2] {'gx','gy'}, use_global_device_ids=true, to_apply=%region_2.3 | all-reduce | flops 16 | bytes 128 | tf_op jit(solution)/shard_map/psum | solution.py:53
  123.4 3.5 multiply_reduce_fusion.14
  126.9 17.1 %psum.255 = f32[8]{0:T(128)S(1)} all-reduce(f32[8]{0:T(128)S(1)} %get-tuple-element.14), channel_id=1, replica_groups=mesh['band'=4,'gx'=4,'gy'=2] {'gx','gy'}, use_global_device_ids=true, to_apply=%region_6.7 | all-reduce | flops 8 | bytes 64 | tf_op jit(solution)/shard_map/psum | solution.py:53
  149.0 2.1 collective-permute-start.48
  151.3 2.2 collective-permute-done.5
  153.6 2.3 collective-permute-start.7
  157.3 2.3 collective-permute-start.51
  161.2 18.5 %psum.256 = f32[8]{0:T(128)S(1)} all-reduce(f32[8]{0:T(128)S(1)} %get-tuple-element.76), channel_id=1, replica_groups=mesh['band'=4,'gx'=4,'gy'=2] {'gx','gy'}, use_global_device_ids=true, to_apply=%region_8.9 | all-reduce | flops 8 | bytes 64 | tf_op jit(solution)/shard_map/psum | solution.py:63
  181.0 17.7 %psum.257 = f32[8]{0:T(128)S(1)} all-reduce(f32[8]{0:T(128)S(1)} %get-tuple-element.74), channel_id=1, replica_groups=mesh['band'=4,'gx'=4,'gy'=2] {'gx','gy'}, use_global_device_ids=true, to_apply=%region_10.11 | all-reduce | flops 8 | bytes 64 | tf_op jit(solution)/shard_map/psum | solution.py:53
  212.8 17.7 %psum.258 = f32[8]{0:T(128)S(1)} all-reduce(f32[8]{0:T(128)S(1)} %get-tuple-element.72), channel_id=1, replica_groups=mesh['band'=4,'gx'=4,'gy'=2] {'gx','gy'}, use_global_device_ids=true, to_apply=%region_12.13 | all-reduce | flops 8 | bytes 64 | tf_op jit(solution)/shard_map/psum | solution.py:63
  234.0 17.5 %psum.259 = f32[8]{0:T(128)S(1)} all-reduce(f32[8]{0:T(128)S(1)} %multiply_reduce_fusion.25), channel_id=1, replica_groups=mesh['band'=4,'gx'=4,'gy'=2] {'gx','gy'}, use_global_device_ids=true, to_apply=%region_14.15 | all-reduce | flops 8 | bytes 64 | tf_op jit(solution)/shard_map/psum | solution.py:53
  259.9 2.2 collective-permute-start.15
  267.2 17.9 %all-reduce.7 = (f32[8]{0:T(128)S(1)}, f32[8]{0:T(128)S(1)}, f32[8]{0:T(128)S(1)}, f32[8]{0:T(128)S(1)}, f32[8]{0:T(128)S(1)}) all-reduce(f32[8]{0:T(128)} %fusion.83, f32[8]{0:T(128)S(1)} %get-tuple-element.15, f32[8]{0:T(128)S(1)} %get-tuple-element.16, ...), channel_id=1, replica_groups=mesh['band'=4,'gx'=4,'gy'=2] {'gx','gy'}, use_global_device_ids=true, to_apply=%region_16.17 | all-reduce | flops 40 | bytes 320 | tf_op jit(solution)/shard_map/psum | solution.py:63
  285.8 3.9 multiply_reduce_fusion.6
  289.7 18.8 %psum.273 = f32[8]{0:T(128)S(1)} all-reduce(f32[8]{0:T(128)S(1)} %get-tuple-element.22), channel_id=1, replica_groups=mesh['band'=4,'gx'=4,'gy'=2] {'gx','gy'}, use_global_device_ids=true, to_apply=%region_42.43 | all-reduce | flops 8 | bytes 64 | tf_op jit(solution)/shard_map/psum | solution.py:53
  321.6 18.2 %psum.274 = f32[8]{0:T(128)S(1)} all-reduce(f32[8]{0:T(128)S(1)} %get-tuple-element.69), channel_id=1, replica_groups=mesh['band'=4,'gx'=4,'gy'=2] {'gx','gy'}, use_global_device_ids=true, to_apply=%region_44.45 | all-reduce | flops 8 | bytes 64 | tf_op jit(solution)/shard_map/psum | solution.py:63
  340.1 18.1 %psum.275 = f32[8]{0:T(128)S(1)} all-reduce(f32[8]{0:T(128)S(1)} %get-tuple-element.67), channel_id=1, replica_groups=mesh['band'=4,'gx'=4,'gy'=2] {'gx','gy'}, use_global_device_ids=true, to_apply=%region_46.47 | all-reduce | flops 8 | bytes 64 | tf_op jit(solution)/shard_map/psum | solution.py:53
  370.9 17.6 %psum.276 = f32[8]{0:T(128)S(1)} all-reduce(f32[8]{0:T(128)S(1)} %get-tuple-element.65), channel_id=1, replica_groups=mesh['band'=4,'gx'=4,'gy'=2] {'gx','gy'}, use_global_device_ids=true, to_apply=%region_48.49 | all-reduce | flops 8 | bytes 64 | tf_op jit(solution)/shard_map/psum | solution.py:63
  388.7 18.7 %psum.277 = f32[8]{0:T(128)S(1)} all-reduce(f32[8]{0:T(128)S(1)} %multiply_reduce_fusion.9), channel_id=1, replica_groups=mesh['band'=4,'gx'=4,'gy'=2] {'gx','gy'}, use_global_device_ids=true, to_apply=%region_50.51 | all-reduce | flops 8 | bytes 64 | tf_op jit(solution)/shard_map/psum | solution.py:53
  419.5 18.2 %all-reduce.6 = (f32[8]{0:T(128)S(1)}, f32[8]{0:T(128)S(1)}, f32[8]{0:T(128)S(1)}) all-reduce(f32[8]{0:T(128)S(1)} %fusion.31, f32[8]{0:T(128)S(1)} %get-tuple-element.12, f32[8]{0:T(128)S(1)} %get-tuple-element.11), channel_id=1, replica_groups=mesh['band'=4,'gx'=4,'gy'=2] {'gx','gy'}, use_global_device_ids=true, to_apply=%region_52.53 | all-reduce | flops 24 | bytes 192 | tf_op jit(solution)/shard_map/psum | solution.py:63
  439.3 18.1 %all-reduce.5 = (f32[8]{0:T(128)S(1)}, f32[8]{0:T(128)S(1)}) all-reduce(f32[8]{0:T(128)S(1)} %get-tuple-element.19, f32[8]{0:T(128)S(1)} %get-tuple-element.21), channel_id=1, replica_groups=mesh['band'=4,'gx'=4,'gy'=2] {'gx','gy'}, use_global_device_ids=true, to_apply=%region_24.25 | all-reduce | flops 16 | bytes 128 | tf_op jit(solution)/shard_map/psum | solution.py:53
  476.8 17.9 %all-reduce.4 = (f32[8]{0:T(128)S(1)}, f32[8]{0:T(128)S(1)}) all-reduce(f32[8]{0:T(128)S(1)} %get-tuple-element.63, f32[8]{0:T(128)S(1)} %get-tuple-element.61), channel_id=1, replica_groups=mesh['band'=4,'gx'=4,'gy'=2] {'gx','gy'}, use_global_device_ids=true, to_apply=%region_26.27 | all-reduce | flops 16 | bytes 128 | tf_op jit(solution)/shard_map/psum | solution.py:63
  494.7 2.5 multiply_reduce_fusion.3
  497.2 18.6 %all-reduce.3 = (f32[8]{0:T(128)S(1)}, f32[8]{0:T(128)S(1)}) all-reduce(f32[8]{0:T(128)S(1)} %get-tuple-element.213, f32[8]{0:T(128)S(1)} %get-tuple-element.57), channel_id=1, replica_groups=mesh['band'=4,'gx'=4,'gy'=2] {'gx','gy'}, use_global_device_ids=true, to_apply=%region_28.29 | all-reduce | flops 16 | bytes 128 | tf_op jit(solution)/shard_map/psum | solution.py:53
  533.6 18.0 %all-reduce.2 = (f32[8]{0:T(128)S(1)}, f32[8]{0:T(128)S(1)}) all-reduce(f32[8]{0:T(128)S(1)} %get-tuple-element.55, f32[8]{0:T(128)S(1)} %get-tuple-element.53), channel_id=1, replica_groups=mesh['band'=4,'gx'=4,'gy'=2] {'gx','gy'}, use_global_device_ids=true, to_apply=%region_30.31 | all-reduce | flops 16 | bytes 128 | tf_op jit(solution)/shard_map/psum | solution.py:63
  554.2 18.2 %all-reduce.1 = (f32[8]{0:T(128)S(1)}, f32[8]{0:T(128)S(1)}) all-reduce(f32[8]{0:T(128)S(1)} %multiply_reduce_fusion.17, f32[8]{0:T(128)S(1)} %multiply_reduce_fusion.1), channel_id=1, replica_groups=mesh['band'=4,'gx'=4,'gy'=2] {'gx','gy'}, use_global_device_ids=true, to_apply=%region_32.33 | all-reduce | flops 16 | bytes 128 | tf_op jit(solution)/shard_map/psum | solution.py:53
  591.0 17.7 %all-reduce = (f32[8]{0:T(128)S(1)}, f32[8]{0:T(128)S(1)}) all-reduce(f32[8]{0:T(128)S(1)} %fusion.57, f32[8]{0:T(128)S(1)} %fusion.5), channel_id=1, replica_groups=mesh['band'=4,'gx'=4,'gy'=2] {'gx','gy'}, use_global_device_ids=true, to_apply=%region_34.35 | all-reduce | flops 16 | bytes 128 | tf_op jit(solution)/shard_map/psum | solution.py:63
  (293 shorter events, 160.1 us)
Async XLA Ops:
  6.5 70.5 %all-reduce.12.cloned.1.call-start = ((), (), s32[]{:S(2)}) async-start(), calls=%async_computation | async-start | bytes 4194304 | tf_op jit(solution)/shard_map/psum | solution.py:28
  81.6 11.0 %collective-permute-start.16 = (f32[8,1,16,128]{3,2,1,0:T(8,128)S(1)}, f32[8,1,16,128]{3,2,1,0:T(8,128)S(1)}, u32[]{:S(2)}, u32[]{:S(2)}) collective-permute-start(f32[8,1,16,128]{3,2,1,0:T(8,128)S(1)} %get-tuple-element.208), channel_id=1, source_target_pairs={{2,0},{4,2},{6,4},{0,6},{3,1},{5,3},{7,5},{1,7},{10,8},{12,10},{14... | collective-permute-start | bytes 196616 | tf_op jit(solution)/shard_map/ppermute | solution.py:21
  84.9 7.7 %collective-permute-start.17 = (f32[8,1,16,128]{3,2,1,0:T(8,128)S(1)}, f32[8,1,16,128]{3,2,1,0:T(8,128)S(1)}, u32[]{:S(2)}, u32[]{:S(2)}) collective-permute-start(f32[8,1,16,128]{3,2,1,0:T(8,128)S(1)} %get-tuple-element.207), channel_id=1, source_target_pairs={{0,2},{2,4},{4,6},{6,0},{1,3},{3,5},{5,7},{7,1},{8,10},{10,12},{12... | collective-permute-start | bytes 196616 | tf_op jit(solution)/shard_map/ppermute | solution.py:18
  84.9 9.3 %collective-permute-start = (f32[8,1,16,128]{3,2,1,0:T(8,128)S(1)}, f32[8,1,16,128]{3,2,1,0:T(8,128)S(1)}, u32[]{:S(2)}, u32[]{:S(2)}) collective-permute-start(f32[8,1,16,128]{3,2,1,0:T(8,128)S(1)} %get-tuple-element.202), channel_id=1, source_target_pairs={{2,0},{4,2},{6,4},{0,6},{3,1},{5,3},{7,5},{1,7},{10,8},{12,10},{14... | collective-permute-start | bytes 196616 | tf_op jit(solution)/shard_map/ppermute | solution.py:21
  88.8 6.1 collective-permute-start.1
  88.8 7.7 %collective-permute-start.32 = (f32[8,1,16,128]{3,2,1,0:T(8,128)S(1)}, f32[8,1,16,128]{3,2,1,0:T(8,128)S(1)}, u32[]{:S(2)}, u32[]{:S(2)}) collective-permute-start(f32[8,1,16,128]{3,2,1,0:T(8,128)S(1)} %get-tuple-element.196), channel_id=1, source_target_pairs={{2,0},{4,2},{6,4},{0,6},{3,1},{5,3},{7,5},{1,7},{10,8},{12,10},{14... | collective-permute-start | bytes 196616 | tf_op jit(solution)/shard_map/ppermute | solution.py:21
  92.6 6.1 collective-permute-start.33
  92.7 7.6 %collective-permute-start.19 = (f32[8,10,1,128]{3,2,1,0:T(1,128)S(1)}, f32[8,10,1,128]{3,2,1,0:T(1,128)S(1)}, u32[]{:S(2)}, u32[]{:S(2)}) collective-permute-start(f32[8,10,1,128]{3,2,1,0:T(1,128)S(1)} %get-tuple-element.116), channel_id=1, source_target_pairs={{0,1},{1,0},{2,3},{3,2},{4,5},{5,4},{6,7},{7,6},{8,9},{9,8},{10,11... | collective-permute-start | bytes 122888 | tf_op jit(solution)/shard_map/ppermute | solution.py:18
  94.2 6.6 %collective-permute-start.18 = (f32[8,10,1,128]{3,2,1,0:T(1,128)S(1)}, f32[8,10,1,128]{3,2,1,0:T(1,128)S(1)}, u32[]{:S(2)}, u32[]{:S(2)}) collective-permute-start(f32[8,10,1,128]{3,2,1,0:T(1,128)S(1)} %get-tuple-element.115), channel_id=1, source_target_pairs={{1,0},{0,1},{3,2},{2,3},{5,4},{4,5},{7,6},{6,7},{9,8},{8,9},{11,10... | collective-permute-start | bytes 122888 | tf_op jit(solution)/shard_map/ppermute | solution.py:21
  94.9 5.9 collective-permute-start.3
  98.8 24.6 %collective-permute-start.35 = (f32[8,10,1,128]{3,2,1,0:T(1,128)S(1)}, f32[8,10,1,128]{3,2,1,0:T(1,128)S(1)}, u32[]{:S(2)}, u32[]{:S(2)}) collective-permute-start(f32[8,10,1,128]{3,2,1,0:T(1,128)S(1)} %get-tuple-element.112), channel_id=1, source_target_pairs={{0,1},{1,0},{2,3},{3,2},{4,5},{5,4},{6,7},{7,6},{8,9},{9,8},{10,11... | collective-permute-start | bytes 122888 | tf_op jit(solution)/shard_map/ppermute | solution.py:18
  100.3 23.1 %collective-permute-start.34 = (f32[8,10,1,128]{3,2,1,0:T(1,128)S(1)}, f32[8,10,1,128]{3,2,1,0:T(1,128)S(1)}, u32[]{:S(2)}, u32[]{:S(2)}) collective-permute-start(f32[8,10,1,128]{3,2,1,0:T(1,128)S(1)} %get-tuple-element.111), channel_id=1, source_target_pairs={{1,0},{0,1},{3,2},{2,3},{5,4},{4,5},{7,6},{6,7},{9,8},{8,9},{11,10... | collective-permute-start | bytes 122888 | tf_op jit(solution)/shard_map/ppermute | solution.py:21
  147.2 6.3 %collective-permute-start.5 = (f32[8,1,16,128]{3,2,1,0:T(8,128)S(1)}, f32[8,1,16,128]{3,2,1,0:T(8,128)S(1)}, u32[]{:S(2)}, u32[]{:S(2)}) collective-permute-start(f32[8,1,16,128]{3,2,1,0:T(8,128)S(1)} %get-tuple-element.189), channel_id=1, source_target_pairs={{0,2},{2,4},{4,6},{6,0},{1,3},{3,5},{5,7},{7,1},{8,10},{10,12},{12... | collective-permute-start | bytes 196616 | tf_op jit(solution)/shard_map/ppermute | solution.py:18
  149.0 6.9 %collective-permute-start.48 = (f32[8,1,16,128]{3,2,1,0:T(8,128)S(1)}, f32[8,1,16,128]{3,2,1,0:T(8,128)S(1)}, u32[]{:S(2)}, u32[]{:S(2)}) collective-permute-start(f32[8,1,16,128]{3,2,1,0:T(8,128)S(1)} %get-tuple-element.172), channel_id=1, source_target_pairs={{2,0},{4,2},{6,4},{0,6},{3,1},{5,3},{7,5},{1,7},{10,8},{12,10},{14... | collective-permute-start | bytes 196616 | tf_op jit(solution)/shard_map/ppermute | solution.py:21
  151.1 6.1 collective-permute-start.49
  153.6 6.0 collective-permute-start.7
  157.3 128.5 %collective-permute-start.51 = (f32[8,10,1,128]{3,2,1,0:T(1,128)S(1)}, f32[8,10,1,128]{3,2,1,0:T(1,128)S(1)}, u32[]{:S(2)}, u32[]{:S(2)}) collective-permute-start(f32[8,10,1,128]{3,2,1,0:T(1,128)S(1)} %get-tuple-element.104), channel_id=1, source_target_pairs={{0,1},{1,0},{2,3},{3,2},{4,5},{5,4},{6,7},{7,6},{8,9},{9,8},{10,11... | collective-permute-start | bytes 122888 | tf_op jit(solution)/shard_map/ppermute | solution.py:18
  199.3 6.1 collective-permute-start.9
  232.4 53.4 %collective-permute-start.50 = (f32[8,10,1,128]{3,2,1,0:T(1,128)S(1)}, f32[8,10,1,128]{3,2,1,0:T(1,128)}, u32[]{:S(2)}, u32[]{:S(2)}) collective-permute-start(f32[8,10,1,128]{3,2,1,0:T(1,128)S(1)} %get-tuple-element.103), channel_id=1, source_target_pairs={{1,0},{0,1},{3,2},{2,3},{5,4},{4,5},{7,6},{6,7},{9,8},{8,9},{11,10... | collective-permute-start | bytes 122888 | tf_op jit(solution)/shard_map/ppermute | solution.py:21
  253.7 6.1 collective-permute-start.13
  309.8 6.1 collective-permute-start.37
  358.4 6.2 collective-permute-start.41
  407.7 6.1 collective-permute-start.45
  459.8 6.3 %collective-permute-start.53 = (f32[8,1,16,128]{3,2,1,0:T(8,128)S(1)}, f32[8,1,16,128]{3,2,1,0:T(8,128)S(1)}, u32[]{:S(2)}, u32[]{:S(2)}) collective-permute-start(f32[8,1,16,128]{3,2,1,0:T(8,128)S(1)} %get-tuple-element.141), channel_id=1, source_target_pairs={{0,2},{2,4},{4,6},{6,0},{1,3},{3,5},{5,7},{7,1},{8,10},{10,12},{12... | collective-permute-start | bytes 196616 | tf_op jit(solution)/shard_map/ppermute | solution.py:18
  461.9 6.4 %collective-permute-start.20 = (f32[8,1,16,128]{3,2,1,0:T(8,128)S(1)}, f32[8,1,16,128]{3,2,1,0:T(8,128)S(1)}, u32[]{:S(2)}, u32[]{:S(2)}) collective-permute-start(f32[8,1,16,128]{3,2,1,0:T(8,128)S(1)} %get-tuple-element.148), channel_id=1, source_target_pairs={{2,0},{4,2},{6,4},{0,6},{3,1},{5,3},{7,5},{1,7},{10,8},{12,10},{14... | collective-permute-start | bytes 196616 | tf_op jit(solution)/shard_map/ppermute | solution.py:21
  463.8 6.1 collective-permute-start.21
  517.0 6.3 %collective-permute-start.25 = (f32[8,1,16,128]{3,2,1,0:T(8,128)S(1)}, f32[8,1,16,128]{3,2,1,0:T(8,128)S(1)}, u32[]{:S(2)}, u32[]{:S(2)}) collective-permute-start(f32[8,1,16,128]{3,2,1,0:T(8,128)S(1)} %get-tuple-element.135), channel_id=1, source_target_pairs={{0,2},{2,4},{4,6},{6,0},{1,3},{3,5},{5,7},{7,1},{8,10},{10,12},{12... | collective-permute-start | bytes 196616 | tf_op jit(solution)/shard_map/ppermute | solution.py:18
  519.0 6.4 %collective-permute-start.56 = (f32[8,1,16,128]{3,2,1,0:T(8,128)S(1)}, f32[8,1,16,128]{3,2,1,0:T(8,128)S(1)}, u32[]{:S(2)}, u32[]{:S(2)}) collective-permute-start(f32[8,1,16,128]{3,2,1,0:T(8,128)S(1)} %get-tuple-element.130), channel_id=1, source_target_pairs={{2,0},{4,2},{6,4},{0,6},{3,1},{5,3},{7,5},{1,7},{10,8},{12,10},{14... | collective-permute-start | bytes 196616 | tf_op jit(solution)/shard_map/ppermute | solution.py:21
  520.9 6.1 collective-permute-start.57
  574.8 6.3 %collective-permute-start.29 = (f32[8,1,16,128]{3,2,1,0:T(8,128)S(1)}, f32[8,1,16,128]{3,2,1,0:T(8,128)S(1)}, u32[]{:S(2)}, u32[]{:S(2)}) collective-permute-start(f32[8,1,16,128]{3,2,1,0:T(8,128)S(1)} %get-tuple-element.127), channel_id=1, source_target_pairs={{0,2},{2,4},{4,6},{6,0},{1,3},{3,5},{5,7},{7,1},{8,10},{10,12},{12... | collective-permute-start | bytes 196616 | tf_op jit(solution)/shard_map/ppermute | solution.py:18
  576.8 6.4 %collective-permute-start.60 = (f32[8,1,16,128]{3,2,1,0:T(8,128)S(1)}, f32[8,1,16,128]{3,2,1,0:T(8,128)S(1)}, u32[]{:S(2)}, u32[]{:S(2)}) collective-permute-start(f32[8,1,16,128]{3,2,1,0:T(8,128)S(1)} %get-tuple-element.122), channel_id=1, source_target_pairs={{2,0},{4,2},{6,4},{0,6},{3,1},{5,3},{7,5},{1,7},{10,8},{12,10},{14... | collective-permute-start | bytes 196616 | tf_op jit(solution)/shard_map/ppermute | solution.py:21
  578.8 6.1 collective-permute-start.61
  (55 other events, 629.8 us)
Sparse Core Ops, SparseCore 0:
  22.4 54.6 all-reduce.11
where the time goes:
time: 619 us; the launch traced here: 618 us
  blocking collectives  345 us (56%)
  waiting for transfers between devices  108 us (17%)
  starting transfers between devices  73.8 us (12%)
  other arithmetic  47.6 us (8%)
  between operations  28.8 us (5%)
  local copies, waits for them, and re-layouts  14.4 us (2%)
    psum x10, blocking collectives, residual_sums(): return lax.psum(partial_products(residual, residual), ('gx', 'gy'))  183 us
    psum x9, blocking collectives, solve_pairs(): curvature = lax.psum(partial_products(direction, image), ('gx', 'gy'))  162 us
    psum x1, waiting for transfers between devices, spread(): return lax.psum(kept, axis)  49.1 us
    ppermute x32, starting transfers between devices, padded_2(): lax.ppermute(lax.slice_in_dim(block, block.shape[dim] - width, None, axis...  43.7 us
    ppermute x32, waiting for transfers between devices, padded_2(): lax.ppermute(lax.slice_in_dim(block, block.shape[dim] - width, None, axis...  36.7 us
    ppermute x32, starting transfers between devices, padded_2(): lax.ppermute(lax.slice_in_dim(block, 0, width, axis=dim), axis, backward)  30 us
    reduce_sum x22, other arithmetic, partial_products(): return jnp.sum(left * right, axis=(1, 2, 3))  29.9 us
    ppermute x32, waiting for transfers between devices, padded_2(): lax.ppermute(lax.slice_in_dim(block, 0, width, axis=dim), axis, backward)  22.6 us
  transfers between devices with their start and end apart: 65, of which 42 were waited for; matrix products, arithmetic and copies ran while one was open for 3% of the time, Pallas kernels for 0%

commit v1 on v0

v1 whole, which is shorter than its diff:
```python
import functools
import math

import jax
import jax.numpy as jnp
from jax import lax
from jax.experimental import pallas as pl
from jax.experimental.pallas import tpu as pltpu
from jax.sharding import PartitionSpec as P

SCREEN = 0.1
DIAGONAL = 6.0 + SCREEN
HALO = 4
NOISE = 1e-6


def apply_row(read, x, ny):
    centre = read(x, 1, ny - 1)
    beside = read(x - 1, 1, ny - 1) + read(x + 1, 1, ny - 1)
    beside = beside + read(x, 0, ny - 2) + read(x, 2, ny)
    lanes = centre.shape[-1]
    beside = beside + pltpu.roll(centre, 1, 2) + pltpu.roll(centre, lanes - 1, 2)
    return DIAGONAL * centre - beside


def cg_kernel(
    n_gx, n_gy, fields_ref, orb_ref, weight_ref, out_ref,
    dens, v1, v2, d2, w, coef, part, parts, send_sem, recv_sem,
):
    ex, ey, nf, nz = fields_ref.shape
    nl = orb_ref.shape[0]
    nx, ny = ex - 2 * HALO, ey - 2 * HALO
    group = n_gx * n_gy
    gx, gy = lax.axis_index("gx"), lax.axis_index("gy")
    me = gx * n_gy + gy
    lane = lax.broadcasted_iota(jnp.int32, (nf, nz), 1)

    def device(index):
        return {"gx": index // n_gy, "gy": lax.rem(index, n_gy)}

    barrier = pltpu.get_barrier_semaphore()

    def greet(off, c):
        pl.semaphore_signal(
            barrier, inc=1, device_id=device(lax.rem(me + off, group)),
            device_id_type=pl.DeviceIdType.MESH,
        )
        return c

    lax.fori_loop(1, group, greet, 0)

    def pack(sums):
        total = jnp.zeros((nf, nz), jnp.float32)
        for m, acc in enumerate(sums):
            value = jnp.sum(acc, axis=1, keepdims=True)
            total = jnp.where(lane == m, jnp.broadcast_to(value, (nf, nz)), total)
        return total

    def unpack(total, m):
        value = jnp.sum(jnp.where(lane == m, total, 0.0), axis=1, keepdims=True)
        return jnp.broadcast_to(value, (nf, nz))

    def copy_to(r, index):
        return pltpu.make_async_remote_copy(
            src_ref=part.at[r], dst_ref=parts.at[r, me],
            send_sem=send_sem.at[r, index], recv_sem=recv_sem.at[r, me],
            device_id=device(index), device_id_type=pl.DeviceIdType.MESH,
        )

    def arrival(r, index):
        return pltpu.make_async_remote_copy(
            src_ref=part.at[r], dst_ref=parts.at[r, index],
            send_sem=send_sem.at[r, index], recv_sem=recv_sem.at[r, index],
            device_id=device(index), device_id_type=pl.DeviceIdType.MESH,
        )

    def all_reduce(r):
        def start(off, c):
            copy_to(r, lax.rem(me + off, group)).start()
            return c

        def finish(off, c):
            index = lax.rem(me + off, group)
            arrival(r, index).wait_recv()
            copy_to(r, index).wait_send()
            return c

        lax.fori_loop(1, group, start, 0)
        parts[r, me] = part[r]
        lax.fori_loop(1, group, finish, 0)
        return lax.fori_loop(1, group, lambda s, t: t + parts[r, s], parts[r, 0])

    def density(i, x, lo, hi):
        return fields_ref[x, lo:hi] * orb_ref[i, x, lo:hi][:, None, :]

    def inner(sums, pairs):
        return tuple(s + jnp.sum(a * b, axis=0) for s, (a, b) in zip(sums, pairs))

    zero = jnp.zeros((nf, nz), jnp.float32)

    def basis(i, c):
        def row0(x, c):
            dens[x] = density(i, x, 0, ey)
            return c

        def row1(x, c):
            v1[i, x] = apply_row(lambda p, lo, hi: dens[p, lo:hi], x + 1, ey)
            return c

        def row2(x, c):
            v2[i, x] = apply_row(lambda p, lo, hi: v1[i, p, lo:hi], x + 1, ey - 2)
            return c

        def products(x, sums):
            b = dens[x + 4, 4 : 4 + ny]
            a1 = v1[i, x + 3, 3 : 3 + ny]
            a2 = v2[i, x + 2, 2 : 2 + ny]
            return inner(sums, ((b, b), (b, a1), (a1, a1), (a1, a2), (a2, a2)))

        lax.fori_loop(0, ex, row0, 0)
        lax.fori_loop(0, ex - 2, row1, 0)
        lax.fori_loop(0, ex - 4, row2, 0)
        part[0, i] = pack(lax.fori_loop(0, nx, products, (zero,) * 5))
        return c

    lax.fori_loop(0, nl, basis, 0)
    pl.semaphore_wait(barrier, group - 1)
    total = all_reduce(0)
    for i in range(nl):
        m0, m1, m2, m3, m4 = (unpack(total[i], m) for m in range(5))
        s0 = m0 / m1
        rr1 = s0 * s0 * m2 - 2.0 * s0 * m1 + m0
        small = rr1 <= NOISE * m0
        b0 = rr1 / m0
        g = 1.0 + b0
        curve = g * g * m1 - 2.0 * g * s0 * m2 + s0 * s0 * m3
        s1 = jnp.where(small, 0.0, rr1 / jnp.where(small, 1.0, curve))
        image2 = g * g * m2 - 2.0 * g * s0 * m3 + s0 * s0 * m4
        rr2 = jnp.maximum(s1 * s1 * image2 - rr1, 0.0)
        b1 = jnp.where(small, 0.0, rr2 / jnp.where(small, 1.0, rr1))
        coef[i, 0], coef[i, 1], coef[i, 2], coef[i, 3] = s0, g, s1, b1

    def second(i, c):
        s0, g, s1, b1 = coef[i, 0], coef[i, 1], coef[i, 2], coef[i, 3]
        cb = 1.0 + b1 * g
        c1 = -(s0 + s1 * g) - b1 * s0
        c2 = s1 * s0

        def row_d(x, c):
            b = density(i, x + 2, 2, ey - 2)
            d2[i, x] = cb * b + c1 * v1[i, x + 1, 1 : ey - 3] + c2 * v2[i, x]
            return c

        def row_w(x, c):
            w[i, x] = apply_row(lambda p, lo, hi: d2[i, p, lo:hi], x + 1, ey - 4)
            return c

        def products(x, sums):
            b = density(i, x + 4, 4, 4 + ny)
            a1 = v1[i, x + 3, 3 : 3 + ny]
            a2 = v2[i, x + 2, 2 : 2 + ny]
            dd = d2[i, x + 2, 2 : 2 + ny]
            ww = w[i, x + 1, 1 : 1 + ny]
            r2 = dd - b1 * (g * b - s0 * a1)
            ad1 = g * a1 - s0 * a2
            aw = apply_row(lambda p, lo, hi: w[i, p, lo:hi], x + 1, ey - 6)
            return inner(
                sums,
                ((r2, r2), (r2, ww), (dd, ww), (ww, ww), (r2, ad1), (ww, ad1), (ww, aw)),
            )

        lax.fori_loop(0, ex - 4, row_d, 0)
        lax.fori_loop(0, ex - 6, row_w, 0)
        part[1, i] = pack(lax.fori_loop(0, nx, products, (zero,) * 7))
        return c

    lax.fori_loop(0, nl, second, 0)
    total = all_reduce(1)
    for i in range(nl):
        rr, rw, dw, ww, ra, wa, waw = (unpack(total[i], m) for m in range(7))
        b1 = coef[i, 3]
        s2 = rr / dw
        rr3 = rr - 2.0 * s2 * rw + s2 * s2 * ww
        small = rr3 <= NOISE * rr
        b2 = rr3 / rr
        r_ar = rw - b1 * ra
        w_ar = ww - b1 * wa
        curve = r_ar + s2 * s2 * waw + b2 * b2 * dw
        curve = curve - 2.0 * s2 * w_ar + 2.0 * b2 * rw - 2.0 * s2 * b2 * ww
        s3 = jnp.where(small, 0.0, rr3 / jnp.where(small, 1.0, curve))
        coef[i, 4], coef[i, 5], coef[i, 6] = s2, b2, s3

    weight = weight_ref[...]

    def combine(i, c):
        s0, g, s1, b1 = coef[i, 0], coef[i, 1], coef[i, 2], coef[i, 3]
        s2, b2, s3 = coef[i, 4], coef[i, 5], coef[i, 6]
        k1 = s1 - s3 * b1
        cb, c1 = s0 + k1 * g, -k1 * s0
        cd, cw = s2 + s3 * (1.0 + b2), -s3 * s2
        cb, c1, cd, cw = cb * weight, c1 * weight, cd * weight, cw * weight

        def row(x, c):
            f = fields_ref[x + 4, 4 : 4 + ny]
            b = f * orb_ref[i, x + 4, 4 : 4 + ny][:, None, :]
            sol = cb * b + c1 * v1[i, x + 3, 3 : 3 + ny]
            sol = sol + cd * d2[i, x + 2, 2 : 2 + ny] + cw * w[i, x + 1, 1 : 1 + ny]
            out_ref[i, x] = -jnp.sum(sol * f, axis=1)
            return c

        lax.fori_loop(0, nx, row, 0)
        return c

    lax.fori_loop(0, nl, combine, 0)


def run_cg(mesh, fields, orbitals, weight):
    n_gx, n_gy = mesh.shape["gx"], mesh.shape["gy"]
    group = n_gx * n_gy
    ex, ey, nf, nz = fields.shape
    nl = orbitals.shape[0]
    vmem = pl.BlockSpec(memory_space=pltpu.VMEM)
    f32 = jnp.float32
    return pl.pallas_call(
        functools.partial(cg_kernel, n_gx, n_gy),
        out_shape=jax.ShapeDtypeStruct((nl, ex - 2 * HALO, ey - 2 * HALO, nz), f32),
        in_specs=[vmem] * 3,
        out_specs=vmem,
        scratch_shapes=[
            pltpu.VMEM((ex, ey, nf, nz), f32),
            pltpu.VMEM((nl, ex - 2, ey - 2, nf, nz), f32),
            pltpu.VMEM((nl, ex - 4, ey - 4, nf, nz), f32),
            pltpu.VMEM((nl, ex - 4, ey - 4, nf, nz), f32),
            pltpu.VMEM((nl, ex - 6, ey - 6, nf, nz), f32),
            pltpu.VMEM((nl, 7, nf, nz), f32),
            pltpu.VMEM((2, nl, nf, nz), f32),
            pltpu.VMEM((2, group, nl, nf, nz), f32),
            pltpu.SemaphoreType.DMA((2, group)),
            pltpu.SemaphoreType.DMA((2, group)),
        ],
        compiler_params=pltpu.CompilerParams(
            collective_id=0, has_side_effects=True, vmem_limit_bytes=48 << 20
        ),
    )(fields, orbitals, weight)


def extend(arrays, axis, dim):
    count = lax.axis_size(axis)
    forward = [(i, (i + 1) % count) for i in range(count)]
    backward = [(target, source) for source, target in forward]
    nz = arrays[0].shape[-1]

    def travel(slabs, pairs):
        flat = jnp.concatenate([s.reshape(-1, nz) for s in slabs])
        flat = lax.ppermute(flat, axis, pairs)
        sizes = [math.prod(s.shape[:-1]) for s in slabs]
        ends = [sum(sizes[: i + 1]) for i in range(len(sizes))]
        return [
            flat[end - size : end].reshape(s.shape)
            for s, size, end in zip(slabs, sizes, ends)
        ]

    lows = travel([lax.slice_in_dim(a, a.shape[dim] - HALO, None, axis=dim) for a in arrays], forward)
    highs = travel([lax.slice_in_dim(a, 0, HALO, axis=dim) for a in arrays], backward)
    return [jnp.concatenate([l, a, h], axis=dim) for l, a, h in zip(lows, arrays, highs)]


def on_device(mesh, local_orbitals, block_orbitals, occupation, owner, block_id):
    n_band = mesh.shape["band"]
    band = lax.axis_index("band")
    turns = owner.shape[0]
    blocks_dev, block = block_orbitals.shape[:2]
    share = block // n_band
    picked = block_orbitals[block_id]
    mine = (owner == band)[:, None, None, None, None]
    picked = jnp.where(mine, picked, 0.0)
    fields = lax.psum_scatter(picked, "band", scatter_dimension=1, tiled=True)
    weights = occupation[owner * blocks_dev + block_id]
    weights = lax.dynamic_slice_in_dim(weights, band * share, share, axis=1)
    fields = fields.reshape((turns * share,) + fields.shape[2:])
    fields = jnp.transpose(fields, (1, 2, 0, 3))
    arrays = extend([fields, local_orbitals[0]], "gx", 0)
    fields, orbital = extend(arrays, "gy", 1)
    orbitals = lax.all_gather(orbital, "band")
    weight = jnp.broadcast_to(weights.reshape(-1, 1), fields.shape[2:])
    result = run_cg(mesh, fields, orbitals, weight)
    return lax.psum_scatter(result, "band", scatter_dimension=0, tiled=True)


def solution(mesh):
    placed = (P("band", "gx", "gy", None), P("band", None, "gx", "gy", None), P(), P(), P())
    return jax.shard_map(
        functools.partial(on_device, mesh),
        mesh=mesh,
        in_specs=placed,
        out_specs=P("band", "gx", "gy", None),
        check_vma=False,
    )
```

time: 619 us -> 177 us (0.29)
  blocking collectives: 345 us -> 8.01 us
  starting transfers between devices: 73.8 us -> 6 us
  other arithmetic: 47.6 us -> 7.21 us
  Pallas kernels: 0 us -> 37.5 us
  between operations: 28.8 us -> 14.2 us
  waiting for transfers between devices: 108 us -> 93.9 us
    psum x19 -> x0, blocking collectives: 345 us -> none  [the longest x10 183 us: residual_sums(): return lax.psum(partial_products(residual, residual), ('gx', 'gy'))]
    ppermute x64 -> x4, starting transfers between devices: 73.8 us -> 5.95 us  [travel(): flat = lax.ppermute(flat, axis, pairs)]
    unnamed x1 -> x3, waiting for transfers between devices: 0.02 us -> 52.4 us
    psum x1 -> x0, waiting for transfers between devices: 49.1 us -> none  [spread(): return lax.psum(kept, axis)]
    pallas_call x0 -> x1, Pallas kernels: none -> 37.5 us  [run_cg(): pl.pallas_call(functools.partial(cg_kernel, n_gx, n_gy), out_shape=jax.Sh...]
    ppermute x64 -> x4, waiting for transfers between devices: 59.3 us -> 22.9 us  [travel(): flat = lax.ppermute(flat, axis, pairs)]
    reduce_sum x24 -> x0, other arithmetic: 33.2 us -> none  [the longest x22 29.9 us: partial_products(): return jnp.sum(left * right, axis=(1, 2, 3))]
    reduce_scatter x0 -> x1, waiting for transfers between devices: none -> 18.7 us  [on_device(): return lax.psum_scatter(result, 'band', scatter_dimension=0, tiled=True)]
  transfers between devices with their start and end apart: 65 -> 6, of which waited for: 42 -> 6; matrix products, arithmetic and copies ran while one was open for 3% -> 2% of each run, Pallas kernels for 0% -> 0%
where the time goes in v1:
time: 177 us
  waiting for transfers between devices  93.9 us (53%)
  Pallas kernels  37.5 us (21%)
  between operations  14.2 us (8%)
  local copies, waits for them, and re-layouts  9.85 us (6%)
  blocking collectives  8.01 us (5%)
  other arithmetic  7.21 us (4%)
  starting transfers between devices  6 us (3%)
    unnamed x3, waiting for transfers between devices  52.4 us
    pallas_call x1, Pallas kernels, run_cg(): pl.pallas_call(functools.partial(cg_kernel, n_gx, n_gy), out_shape=jax.Sh...  37.5 us
    ppermute x4, waiting for transfers between devices, travel(): flat = lax.ppermute(flat, axis, pairs)  22.9 us
    reduce_scatter x1, waiting for transfers between devices, on_device(): return lax.psum_scatter(result, 'band', scatter_dimension=0, tiled=True)  18.7 us
    all_gather x1, blocking collectives, on_device(): orbitals = lax.all_gather(orbital, 'band')  8.01 us
    ppermute x4, starting transfers between devices, travel(): flat = lax.ppermute(flat, axis, pairs)  5.95 us
  transfers between devices with their start and end apart: 6, of which 6 were waited for; matrix products, arithmetic and copies ran while one was open for 2% of the time, Pallas kernels for 0%

profile of v1, /device:TPU:0, one launch (start us, length us, event | category | flops | bytes accessed | tf_op | source)
XLA Modules:
  0.0 176.7 jit_solution(14548237383909288607)
XLA Ops:
  6.5 0.8 compare_select_fusion
  7.4 0.8 broadcast_compare_fusion
  8.2 0.6 pad_clamp_fusion
  8.8 2.0 %gather_fusion = f32[4,8,8,16,128]{4,3,2,1,0:T(8,128)} fusion(f32[6,8,8,16,128]{4,3,2,1,0:T(8,128)S(1)} %copy-done, s32[1024]{0:T(1024)S(1)} %get-tuple-element.16), kind=kCustom, calls=%fused_computation | custom fusion | bytes 4194320 | tf_op jit(solution)/shard_map/gather | solution.py:274
  10.8 3.3 %broadcast_select_fusion = f32[4,8,8,16,128]{4,3,2,1,0:T(8,128)} fusion(f32[4,8,8,16,128]{4,3,2,1,0:T(8,128)} %gather_fusion, pred[4]{0:T(512)(128)(4,1)S(1)} %broadcast_compare_fusion), kind=kLoop, calls=%fused_computation.3 | loop fusion | flops 524288 | bytes 4194308 | tf_op jit(solution)/shard_map/jit(_where)/select_n | solution.py:276
  14.1 0.6 copy-done.7
  14.7 0.6 dynamic-slice
  16.0 52.3 %all-reduce.3.cloned.1.call-done = f32[4,8,8,16,128]{4,3,2,1,0:T(8,128)} async-done(((f32[4,8,8,16,128]{4,3,2,1,0:T(8,128)}), f32[4,8,8,16,128]{4,3,2,1,0:T(8,128)}) %all-reduce.3.cloned.1.call-update) | async-done | bytes 2097168
  68.3 1.1 constant_dynamic-slice_fusion
  69.4 0.4 copy.10
  69.9 1.5 collective-permute-start
  71.5 2.4 %collective-permute-start.1 = (f32[576,128]{1,0:T(8,128)S(1)}, f32[576,128]{1,0:T(8,128)S(1)}, u32[]{:S(2)}, u32[]{:S(2)}) collective-permute-start(f32[576,128]{1,0:T(8,128)S(1)} %pad_maximum_fusion.2), channel_id=1, source_target_pairs={{2,0},{4,2},{6,4},{0,6},{3,1},{5,3},{7,5},{1,7},{10,8},{12,10},{14... | collective-permute-start | bytes 884744 | tf_op jit(solution)/shard_map/ppermute | solution.py:255
  73.8 7.8 %collective-permute-done = f32[576,128]{1,0:T(8,128)S(1)} collective-permute-done((f32[576,128]{1,0:T(8,128)S(1)}, f32[576,128]{1,0:T(8,128)S(1)}, u32[]{:S(2)}, u32[]{:S(2)}) %collective-permute-start) | collective-permute-done | bytes 294944 | tf_op jit(solution)/shard_map/ppermute | solution.py:255
  81.7 4.5 %collective-permute-done.1 = f32[576,128]{1,0:T(8,128)S(1)} collective-permute-done((f32[576,128]{1,0:T(8,128)S(1)}, f32[576,128]{1,0:T(8,128)S(1)}, u32[]{:S(2)}, u32[]{:S(2)}) %collective-permute-start.1) | collective-permute-done | bytes 294944 | tf_op jit(solution)/shard_map/ppermute | solution.py:255
  86.3 0.6 copy-done.3
  87.0 0.7 pad_maximum_fusion.3
  87.7 1.5 collective-permute-start.2
  89.2 0.7 pad_maximum_fusion.4
  89.9 0.6 collective-permute-start.3
  90.6 0.7 gather_fusion.1
  91.2 0.1 constant_dynamic-slice_fusion.1
  91.3 0.1 broadcast_in_dim.30
  91.4 6.6 %collective-permute-done.2 = f32[576,128]{1,0:T(8,128)} collective-permute-done((f32[576,128]{1,0:T(8,128)}, f32[576,128]{1,0:T(8,128)}, u32[]{:S(2)}, u32[]{:S(2)}) %collective-permute-start.2) | collective-permute-done | bytes 294944 | tf_op jit(solution)/shard_map/ppermute | solution.py:255
  98.0 0.8 slice.78
  98.8 4.0 %collective-permute-done.3 = f32[576,128]{1,0:T(8,128)} collective-permute-done((f32[576,128]{1,0:T(8,128)}, f32[576,128]{1,0:T(8,128)}, u32[]{:S(2)}, u32[]{:S(2)}) %collective-permute-start.3) | collective-permute-done | bytes 294944 | tf_op jit(solution)/shard_map/ppermute | solution.py:255
  102.7 0.8 slice.79
  103.5 8.0 %all-gather = f32[64,24,128]{2,1,0:T(8,128)S(1)} all-gather(f32[16,24,128]{2,1,0:T(8,128)S(1)} %pad_maximum_fusion.8), channel_id=2, replica_groups=mesh['band'=4,'gx'=4,'gy'=2] {'band'}, dimensions={0}, use_global_device_ids=true | all-gather | bytes 983040 | tf_op jit(solution)/shard_map/all_gather | solution.py:284
  111.5 1.0 slice.76
  112.5 1.0 slice.77
  113.5 0.1 pad_maximum_fusion.fields_ref
  113.7 37.5 %shard_map.55 = f32[4,8,16,128]{3,2,1,0:T(8,128)} custom-call(f32[16,24,8,128]{3,2,1,0:T(8,128)S(1)} %pad_maximum_fusion.fields_ref, f32[4,16,24,128]{3,2,1,0:T(8,128)S(1)} %bitcast.28, f32[8,128]{1,0:T(8,128)S(1)} %broadcast_in_dim.31.weight_ref), custom_call_target="tpu_custom_call" | custom-call | tf_op jit(solution)/shard_map/pallas_call | solution.py:224
  151.3 18.7 %reduce-scatter.5.cloned.1.call-done = f32[1,8,16,128]{3,2,1,0:T(8,128)} async-done(((f32[4,8,16,128]{3,2,1,0:T(8,128)}), f32[1,8,16,128]{3,2,1,0:T(8,128)}) %reduce-scatter.5.cloned.1.call-update) | async-done | bytes 65552 | tf_op jit(solution)/shard_map/reduce_scatter | solution.py:287
  (31 shorter events, 0.5 us)
Async XLA Ops:
  6.5 2.2 %copy-start = (f32[6,8,8,16,128]{4,3,2,1,0:T(8,128)S(1)}, f32[6,8,8,16,128]{4,3,2,1,0:T(8,128)}, u32[]{:S(2)}) copy-start(f32[6,8,8,16,128]{4,3,2,1,0:T(8,128)} %param.6) | copy-start | bytes 9437188
  6.5 61.8 %all-reduce.3.cloned.1.call-start = ((), (), s32[]{:S(2)}) async-start(), calls=%async_computation.2 | async-start | bytes 4194304
  14.0 0.7 copy-start.7
  14.1 1.9 %copy-start.5 = (f32[1,8,16,128]{3,2,1,0:T(8,128)S(1)}, f32[1,8,16,128]{3,2,1,0:T(8,128)}, u32[]{:S(2)}) copy-start(f32[1,8,16,128]{3,2,1,0:T(8,128)} %param.5) | copy-start | bytes 196612
  14.1 155.8 %reduce-scatter.5.cloned.1.call-start = ((), (), s32[]{:S(2)}) async-start(), calls=%async_computation.1 | async-start | bytes 327680 | tf_op jit(solution)/shard_map/reduce_scatter | solution.py:287
  69.8 16.5 %copy-start.1 = (f32[4,2,8,16,128]{4,1,0,3,2:T(2,128)}, f32[4,2,8,16,128]{4,1,0,3,2:T(2,128)S(1)}, u32[]{:S(2)}) copy-start(f32[4,2,8,16,128]{4,1,0,3,2:T(2,128)S(1)} %copy.10) | copy-start | bytes 1572868
  69.9 11.8 %collective-permute-start = (f32[576,128]{1,0:T(8,128)S(1)}, f32[576,128]{1,0:T(8,128)S(1)}, u32[]{:S(2)}, u32[]{:S(2)}) collective-permute-start(f32[576,128]{1,0:T(8,128)S(1)} %pad_maximum_fusion.1), channel_id=1, source_target_pairs={{0,2},{2,4},{4,6},{6,0},{1,3},{3,5},{5,7},{7,1},{8,10},{10,12},{12... | collective-permute-start | bytes 884744 | tf_op jit(solution)/shard_map/ppermute | solution.py:255
  71.4 19.0 %copy-start.6 = (f32[24,8]{0,1:T(8,128)S(1)}, f32[24,8]{0,1:T(8,128)}, u32[]{:S(2)}) copy-start(f32[24,8]{0,1:T(8,128)} %param.7) | copy-start | bytes 2308
  71.5 14.8 %collective-permute-start.1 = (f32[576,128]{1,0:T(8,128)S(1)}, f32[576,128]{1,0:T(8,128)S(1)}, u32[]{:S(2)}, u32[]{:S(2)}) collective-permute-start(f32[576,128]{1,0:T(8,128)S(1)} %pad_maximum_fusion.2), channel_id=1, source_target_pairs={{2,0},{4,2},{6,4},{0,6},{3,1},{5,3},{7,5},{1,7},{10,8},{12,10},{14... | collective-permute-start | bytes 884744 | tf_op jit(solution)/shard_map/ppermute | solution.py:255
  86.2 0.7 copy-start.3
  87.7 10.3 %collective-permute-start.2 = (f32[576,128]{1,0:T(8,128)}, f32[576,128]{1,0:T(8,128)}, u32[]{:S(2)}, u32[]{:S(2)}) collective-permute-start(f32[576,128]{1,0:T(8,128)} %pad_maximum_fusion.3), channel_id=1, source_target_pairs={{0,1},{1,0},{2,3},{3,2},{4,5},{5,4},{6,7},{7,6},{8,9},{9,8},{10,11... | collective-permute-start | bytes 884744 | tf_op jit(solution)/shard_map/ppermute | solution.py:255
  89.9 12.8 %collective-permute-start.3 = (f32[576,128]{1,0:T(8,128)}, f32[576,128]{1,0:T(8,128)}, u32[]{:S(2)}, u32[]{:S(2)}) collective-permute-start(f32[576,128]{1,0:T(8,128)} %pad_maximum_fusion.4), channel_id=1, source_target_pairs={{1,0},{0,1},{3,2},{2,3},{5,4},{4,5},{7,6},{6,7},{9,8},{8,9},{11,10... | collective-permute-start | bytes 884744 | tf_op jit(solution)/shard_map/ppermute | solution.py:255
  91.4 22.1 %copy-start.2 = (f32[4,2,8,16,128]{4,1,0,3,2:T(2,128)S(1)}, f32[4,2,8,16,128]{4,1,0,3,2:T(2,128)}, u32[]{:S(2)}) copy-start(f32[4,2,8,16,128]{4,1,0,3,2:T(2,128)} %copy-done.1) | copy-start | bytes 1572868
  91.4 22.1 %copy-start.4 = (f32[512,128]{1,0:T(8,128)S(1)}, f32[512,128]{1,0:T(8,128)}, u32[]{:S(2)}) copy-start(f32[512,128]{1,0:T(8,128)} %copy-done.3) | copy-start | bytes 786436
Sparse Core Ops, SparseCore 0:
  14.2 54.0 all-reduce.2
  151.4 18.4 reduce-scatter.4

commit v2 on v1

--- a/solution.py
+++ b/solution.py
@@ -1,5 +1,4 @@
 import functools
-import math
 
 import jax
 import jax.numpy as jnp
@@ -11,6 +10,7 @@
 SCREEN = 0.1
 DIAGONAL = 6.0 + SCREEN
 HALO = 4
+CORES = 2
 NOISE = 1e-6
 
 
@@ -24,19 +24,32 @@
 
 
 def cg_kernel(
-    n_gx, n_gy, fields_ref, orb_ref, weight_ref, out_ref,
+    n_band, n_gx, n_gy, owner_ref, picked_ref, local_ref, weight_ref, out_ref,
+    fields_ref, orb_ref, from_mate, combined, from_far, results, results_in,
     dens, v1, v2, d2, w, coef, part, parts, send_sem, recv_sem,
+    mate_sem, far_sem, orb_sem, halo_sem, result_sem,
 ):
     ex, ey, nf, nz = fields_ref.shape
     nl = orb_ref.shape[0]
+    turns, n_chip, cores, share = picked_ref.shape[:4]
+    per_band = nl // n_band
     nx, ny = ex - 2 * HALO, ey - 2 * HALO
     group = n_gx * n_gy
-    gx, gy = lax.axis_index("gx"), lax.axis_index("gy")
+    band, gx, gy = (lax.axis_index(axis) for axis in ("band", "gx", "gy"))
     me = gx * n_gy + gy
+    chip, core = band // cores, lax.rem(band, cores)
+    mate = chip * cores + 1 - core
     lane = lax.broadcasted_iota(jnp.int32, (nf, nz), 1)
+    inside_x, inside_y = pl.ds(HALO, nx), pl.ds(HALO, ny)
 
     def device(index):
         return {"gx": index // n_gy, "gy": lax.rem(index, n_gy)}
+
+    def remote(src, dst, sems, target):
+        return pltpu.make_async_remote_copy(
+            src_ref=src, dst_ref=dst, send_sem=sems[0], recv_sem=sems[1],
+            device_id=target, device_id_type=pl.DeviceIdType.MESH,
+        )
 
     barrier = pltpu.get_barrier_semaphore()
 
@@ -47,7 +60,99 @@
         )
         return c
 
+    def greet_band(off, c):
+        pl.semaphore_signal(
+            barrier, inc=1, device_id={"band": lax.rem(band + off, n_band)},
+            device_id_type=pl.DeviceIdType.MESH,
+        )
+        return c
+
     lax.fori_loop(1, group, greet, 0)
+    lax.fori_loop(1, n_band, greet_band, 0)
+    pl.semaphore_wait(barrier, group + n_band - 2)
+
+    to_mate = [
+        remote(
+            picked_ref.at[t, :, 1 - core], from_mate.at[t],
+            (mate_sem.at[0, t], mate_sem.at[1, t]), {"band": mate},
+        )
+        for t in range(turns)
+    ]
+    for copy in to_mate:
+        copy.start()
+    orb_copies = [
+        remote(
+            local_ref, orb_ref.at[pl.ds(band * per_band, per_band), inside_x, inside_y],
+            (orb_sem.at[0, off], orb_sem.at[1, off]), {"band": lax.rem(band + off, n_band)},
+        )
+        for off in range(1, n_band)
+    ]
+    for copy in orb_copies:
+        copy.start()
+    orb_ref[pl.ds(band * per_band, per_band), inside_x, inside_y] = local_ref[...]
+    far = []
+    for t in range(turns):
+        to_mate[t].wait()
+        by_mate = owner_ref[t] == mate
+        for off in range(1, n_chip):
+            there = lax.rem(chip + off, n_chip)
+            combined[off - 1, t] = jnp.where(
+                by_mate, from_mate[t, there], picked_ref[t, there, core]
+            )
+            copy = remote(
+                combined.at[off - 1, t], from_far.at[off - 1, t],
+                (far_sem.at[0, off - 1, t], far_sem.at[1, off - 1, t]),
+                {"band": there * cores + core},
+            )
+            copy.start()
+            far.append((t, copy))
+
+    def halo(ref, lead, which):
+        def along_x(lo, n, dst, target, k):
+            src = ref.at[lead + (pl.ds(lo, n), inside_y)]
+            dst = ref.at[lead + (pl.ds(dst, n), inside_y)]
+            return remote(src, dst, (halo_sem.at[0, which, k], halo_sem.at[1, which, k]), target)
+
+        def along_y(lo, n, dst, target, k):
+            src = ref.at[lead + (slice(None), pl.ds(lo, n))]
+            dst = ref.at[lead + (slice(None), pl.ds(dst, n))]
+            return remote(src, dst, (halo_sem.at[0, which, k], halo_sem.at[1, which, k]), target)
+
+        up, down = {"gx": lax.rem(gx + 1, n_gx)}, {"gx": lax.rem(gx + n_gx - 1, n_gx)}
+        right, left = {"gy": lax.rem(gy + 1, n_gy)}, {"gy": lax.rem(gy + n_gy - 1, n_gy)}
+        return (
+            [along_x(nx, HALO, 0, up, 0), along_x(HALO, HALO, HALO + nx, down, 1)],
+            [along_y(ny, HALO, 0, right, 2), along_y(HALO, HALO, HALO + ny, left, 3)],
+        )
+
+    for copy in orb_copies:
+        copy.wait()
+    orb_x, orb_y = halo(orb_ref, (slice(None),), 0)
+    field_x, field_y = halo(fields_ref, (), 1)
+    for copy in orb_x:
+        copy.start()
+    for copy in orb_x:
+        copy.wait()
+    for copy in orb_y:
+        copy.start()
+    for t in range(turns):
+        for turn, copy in far:
+            if turn == t:
+                copy.wait()
+        who = owner_ref[t]
+        value = jnp.where(who == mate, from_mate[t, chip], picked_ref[t, chip, core])
+        for off in range(1, n_chip):
+            there = lax.rem(chip + n_chip - off, n_chip)
+            value = jnp.where(who // cores == there, from_far[off - 1, t], value)
+        for s in range(share):
+            fields_ref[inside_x, inside_y, t * share + s, :] = value[s]
+    for copies in (field_x, field_y):
+        for copy in copies:
+            copy.start()
+        for copy in copies:
+            copy.wait()
+    for copy in orb_y:
+        copy.wait()
 
     def pack(sums):
         total = jnp.zeros((nf, nz), jnp.float32)
@@ -91,7 +196,7 @@
         return lax.fori_loop(1, group, lambda s, t: t + parts[r, s], parts[r, 0])
 
     def density(i, x, lo, hi):
-        return fields_ref[x, lo:hi] * orb_ref[i, x, lo:hi][:, None, :]
+        return fields_ref[x, lo:hi] * orb_ref[i, x, lo:hi]
 
     def inner(sums, pairs):
         return tuple(s + jnp.sum(a * b, axis=0) for s, (a, b) in zip(sums, pairs))
@@ -124,7 +229,6 @@
         return c
 
     lax.fori_loop(0, nl, basis, 0)
-    pl.semaphore_wait(barrier, group - 1)
     total = all_reduce(0)
     for i in range(nl):
         m0, m1, m2, m3, m4 = (unpack(total[i], m) for m in range(5))
@@ -192,7 +296,7 @@
 
     weight = weight_ref[...]
 
-    def combine(i, c):
+    def combine(i):
         s0, g, s1, b1 = coef[i, 0], coef[i, 1], coef[i, 2], coef[i, 3]
         s2, b2, s3 = coef[i, 4], coef[i, 5], coef[i, 6]
         k1 = s1 - s3 * b1
@@ -202,31 +306,60 @@
 
         def row(x, c):
             f = fields_ref[x + 4, 4 : 4 + ny]
-            b = f * orb_ref[i, x + 4, 4 : 4 + ny][:, None, :]
+            b = f * orb_ref[i, x + 4, 4 : 4 + ny]
             sol = cb * b + c1 * v1[i, x + 3, 3 : 3 + ny]
             sol = sol + cd * d2[i, x + 2, 2 : 2 + ny] + cw * w[i, x + 1, 1 : 1 + ny]
-            out_ref[i, x] = -jnp.sum(sol * f, axis=1)
+            results[i, x] = -jnp.sum(sol * f, axis=1)
             return c
 
         lax.fori_loop(0, nx, row, 0)
+
+    def to_band(off):
+        target = lax.rem(band + off, n_band)
+        return remote(
+            results.at[pl.ds(target * per_band, per_band)], results_in.at[off - 1],
+            (result_sem.at[0, off - 1], result_sem.at[1, off - 1]), {"band": target},
+        )
+
+    def send_results(off, c):
+        target = lax.rem(band + off, n_band)
+        for k in range(per_band):
+            combine(target * per_band + k)
+        to_band(off).start()
         return c
 
-    lax.fori_loop(0, nl, combine, 0)
-
-
-def run_cg(mesh, fields, orbitals, weight):
-    n_gx, n_gy = mesh.shape["gx"], mesh.shape["gy"]
+    lax.fori_loop(1, n_band, send_results, 0)
+    for k in range(per_band):
+        combine(band * per_band + k)
+    value = results[pl.ds(band * per_band, per_band)]
+    for off in range(1, n_band):
+        to_band(off).wait()
+        value = value + results_in[off - 1]
+    out_ref[...] = value
+
+
+def run(mesh, owner, picked, local, weight):
+    n_band, n_gx, n_gy = (mesh.shape[axis] for axis in ("band", "gx", "gy"))
     group = n_gx * n_gy
-    ex, ey, nf, nz = fields.shape
-    nl = orbitals.shape[0]
+    turns, n_chip, _, share, nx, ny, nz = picked.shape
+    ex, ey, nf = nx + 2 * HALO, ny + 2 * HALO, turns * share
+    per_band = local.shape[0]
+    nl = per_band * n_band
     vmem = pl.BlockSpec(memory_space=pltpu.VMEM)
     f32 = jnp.float32
     return pl.pallas_call(
-        functools.partial(cg_kernel, n_gx, n_gy),
-        out_shape=jax.ShapeDtypeStruct((nl, ex - 2 * HALO, ey - 2 * HALO, nz), f32),
-        in_specs=[vmem] * 3,
+        functools.partial(cg_kernel, n_band, n_gx, n_gy),
+        out_shape=jax.ShapeDtypeStruct((per_band, nx, ny, nz), f32),
+        in_specs=[pl.BlockSpec(memory_space=pltpu.SMEM)] + [vmem] * 3,
         out_specs=vmem,
         scratch_shapes=[
+            pltpu.VMEM((ex, ey, nf, nz), f32),
+            pltpu.VMEM((nl, ex, ey, 1, nz), f32),
+            pltpu.VMEM((turns, n_chip, share, nx, ny, nz), f32),
+            pltpu.VMEM((n_chip - 1, turns, share, nx, ny, nz), f32),
+            pltpu.VMEM((n_chip - 1, turns, share, nx, ny, nz), f32),
+            pltpu.VMEM((nl, nx, ny, nz), f32),
+            pltpu.VMEM((n_band - 1, per_band, nx, ny, nz), f32),
             pltpu.VMEM((ex, ey, nf, nz), f32),
             pltpu.VMEM((nl, ex - 2, ey - 2, nf, nz), f32),
             pltpu.VMEM((nl, ex - 4, ey - 4, nf, nz), f32),
@@ -237,54 +370,30 @@
             pltpu.VMEM((2, group, nl, nf, nz), f32),
             pltpu.SemaphoreType.DMA((2, group)),
             pltpu.SemaphoreType.DMA((2, group)),
+            pltpu.SemaphoreType.DMA((2, turns)),
+            pltpu.SemaphoreType.DMA((2, n_chip - 1, turns)),
+            pltpu.SemaphoreType.DMA((2, n_band)),
+            pltpu.SemaphoreType.DMA((2, 2, 4)),
+            pltpu.SemaphoreType.DMA((2, n_band - 1)),
         ],
         compiler_params=pltpu.CompilerParams(
-            collective_id=0, has_side_effects=True, vmem_limit_bytes=48 << 20
+            collective_id=0, has_side_effects=True, vmem_limit_bytes=50 << 20
         ),
-    )(fields, orbitals, weight)
-
-
-def extend(arrays, axis, dim):
-    count = lax.axis_size(axis)
-    forward = [(i, (i + 1) % count) for i in range(count)]
-    backward = [(target, source) for source, target in forward]
-    nz = arrays[0].shape[-1]
-
-    def travel(slabs, pairs):
-        flat = jnp.concatenate([s.reshape(-1, nz) for s in slabs])
-        flat = lax.ppermute(flat, axis, pairs)
-        sizes = [math.prod(s.shape[:-1]) for s in slabs]
-        ends = [sum(sizes[: i + 1]) for i in range(len(sizes))]
-        return [
-            flat[end - size : end].reshape(s.shape)
-            for s, size, end in zip(slabs, sizes, ends)
-        ]
-
-    lows = travel([lax.slice_in_dim(a, a.shape[dim] - HALO, None, axis=dim) for a in arrays], forward)
-    highs = travel([lax.slice_in_dim(a, 0, HALO, axis=dim) for a in arrays], backward)
-    return [jnp.concatenate([l, a, h], axis=dim) for l, a, h in zip(lows, arrays, highs)]
+    )(owner, picked, local, weight)
 
 
 def on_device(mesh, local_orbitals, block_orbitals, occupation, owner, block_id):
     n_band = mesh.shape["band"]
     band = lax.axis_index("band")
     turns = owner.shape[0]
-    blocks_dev, block = block_orbitals.shape[:2]
+    blocks_dev, block, nx, ny, nz = block_orbitals.shape
     share = block // n_band
     picked = block_orbitals[block_id]
-    mine = (owner == band)[:, None, None, None, None]
-    picked = jnp.where(mine, picked, 0.0)
-    fields = lax.psum_scatter(picked, "band", scatter_dimension=1, tiled=True)
+    picked = picked.reshape(turns, n_band // CORES, CORES, share, nx, ny, nz)
     weights = occupation[owner * blocks_dev + block_id]
     weights = lax.dynamic_slice_in_dim(weights, band * share, share, axis=1)
-    fields = fields.reshape((turns * share,) + fields.shape[2:])
-    fields = jnp.transpose(fields, (1, 2, 0, 3))
-    arrays = extend([fields, local_orbitals[0]], "gx", 0)
-    fields, orbital = extend(arrays, "gy", 1)
-    orbitals = lax.all_gather(orbital, "band")
-    weight = jnp.broadcast_to(weights.reshape(-1, 1), fields.shape[2:])
-    result = run_cg(mesh, fields, orbitals, weight)
-    return lax.psum_scatter(result, "band", scatter_dimension=0, tiled=True)
+    weight = jnp.broadcast_to(weights.reshape(-1, 1), (turns * share, nz))
+    return run(mesh, owner, picked, local_orbitals[:, :, :, None, :], weight)
 
 
 def solution(mesh):

time: 177 us -> 90.8 us (0.51)
  waiting for transfers between devices: 93.9 us -> 0 us
  Pallas kernels: 37.5 us -> 83.8 us
  between operations: 14.2 us -> 0.02 us
  blocking collectives: 8.01 us -> 0 us
  other arithmetic: 7.21 us -> 0.83 us
  starting transfers between devices: 6 us -> 0 us
  local copies, waits for them, and re-layouts: 9.85 us -> 5.95 us
    unnamed x3 -> x0, waiting for transfers between devices: 52.4 us -> none
    pallas_call x1, Pallas kernels: 37.5 us -> 83.8 us  [run(): pl.pallas_call(functools.partial(cg_kernel, n_band, n_gx, n_gy), out_shap...]
    ppermute x4 -> x0, waiting for transfers between devices: 22.9 us -> none  [travel(): flat = lax.ppermute(flat, axis, pairs)]
    reduce_scatter x1 -> x0, waiting for transfers between devices: 18.7 us -> none  [on_device(): return lax.psum_scatter(result, 'band', scatter_dimension=0, tiled=True)]
    all_gather x1 -> x0, blocking collectives: 8.01 us -> none  [on_device(): orbitals = lax.all_gather(orbital, 'band')]
    ppermute x4 -> x0, starting transfers between devices: 5.95 us -> none  [travel(): flat = lax.ppermute(flat, axis, pairs)]
    slice x10 -> x0, local copies, waits for them, and re-layouts: 3.54 us -> none  [the longest x8 3.5 us: travel(): flat[end - size:end].reshape(s.shape)]
    select_n x1 -> x0, other arithmetic: 3.28 us -> none  [on_device(): picked = jnp.where(mine, picked, 0.0)]
  transfers between devices with their start and end apart: 6 -> 0, of which waited for: 6 -> 0; matrix products, arithmetic and copies ran while one was open for 2% -> 0% of each run, Pallas kernels for 0% -> 0%
where the time goes in v2:
time: 90.8 us; the launch traced here: 90.6 us
  Pallas kernels  83.8 us (92%)
  local copies, waits for them, and re-layouts  5.95 us (7%)
    pallas_call x1, Pallas kernels, run(): pl.pallas_call(functools.partial(cg_kernel, n_band, n_gx, n_gy), out_shap...  83.8 us
    unnamed x10, local copies, waits for them, and re-layouts  3.13 us
    gather x1, local copies, waits for them, and re-layouts, on_device(): picked = block_orbitals[block_id]  2.02 us

profile of v2, /device:TPU:0, one launch (start us, length us, event | category | flops | bytes accessed | tf_op | source)
XLA Modules:
  0.0 90.6 jit_solution(18068286939462017596)
XLA Ops:
  0.0 0.0 copy-start
  0.0 0.8 compare_select_fusion
  0.8 0.9 copy.7
  1.7 0.6 gather_fusion.1
  2.3 0.1 constant_dynamic-slice_fusion
  2.4 0.1 broadcast_in_dim.19
  2.5 0.1 broadcast_in_dim.20.weight_ref
  2.5 0.0 copy-done
  2.5 0.0 copy-start.2
  2.5 0.0 copy-start.3
  2.5 2.0 %gather_fusion = f32[4,8,8,16,128]{4,3,2,1,0:T(8,128)} fusion(f32[6,8,8,16,128]{4,3,2,1,0:T(8,128)S(1)} %copy-done, s32[1024]{0:T(1024)S(1)} %get-tuple-element.8), kind=kCustom, calls=%fused_computation | custom fusion | bytes 4194320 | tf_op jit(solution)/shard_map/gather | solution.py:391
  4.6 0.0 copy-done.2
  4.6 0.0 copy-done.3
  4.6 0.0 copy-start.1
  4.6 1.6 %copy-done.1 = f32[4,8,8,16,128]{4,3,2,1,0:T(8,128)S(1)} copy-done((f32[4,8,8,16,128]{4,3,2,1,0:T(8,128)S(1)}, f32[4,8,8,16,128]{4,3,2,1,0:T(8,128)}, u32[]{:S(2)}) %copy-start.1) | copy-done | bytes 2097176
  6.2 83.8 %shard_map.55 = f32[1,8,16,128]{3,2,1,0:T(8,128)S(1)} custom-call(s32[4]{0:T(128)S(1)} %copy-done.3, f32[4,2,2,2,8,16,128]{6,5,4,3,2,1,0:T(8,128)S(1)} %bitcast.2, f32[1,8,16,1,128]{4,3,2,1,0:T(1,128)S(1)} %bitcast.3, f32[8,128]{1,0:T(8,128)S(1)} %broadcast_in_dim.20.weight_ref), custom_call_target="tpu_custom_call" | custom-call | tf_op jit(solution)/shard_map/pallas_call | solution.py:350
  89.9 0.6 copy.9
  (1 shorter events, 0.0 us)
Async XLA Ops:
  0.0 2.5 %copy-start = (f32[6,8,8,16,128]{4,3,2,1,0:T(8,128)S(1)}, f32[6,8,8,16,128]{4,3,2,1,0:T(8,128)}, u32[]{:S(2)}) copy-start(f32[6,8,8,16,128]{4,3,2,1,0:T(8,128)} %param.6) | copy-start | bytes 9437188
  2.5 2.0 %copy-start.2 = (f32[1,8,16,128]{3,2,1,0:T(8,128)S(1)}, f32[1,8,16,128]{3,2,1,0:T(8,128)}, u32[]{:S(2)}) copy-start(f32[1,8,16,128]{3,2,1,0:T(8,128)} %param.5) | copy-start | bytes 196612
  2.5 2.0 %copy-start.3 = (s32[4]{0:T(128)S(1)}, s32[4]{0:T(128)}, u32[]{:S(2)}) copy-start(s32[4]{0:T(128)} %owner_ref.1) | copy-start | bytes 52
  4.6 1.6 %copy-start.1 = (f32[4,8,8,16,128]{4,3,2,1,0:T(8,128)S(1)}, f32[4,8,8,16,128]{4,3,2,1,0:T(8,128)}, u32[]{:S(2)}) copy-start(f32[4,8,8,16,128]{4,3,2,1,0:T(8,128)} %gather_fusion) | copy-start | bytes 6291460

commit v3 on v2

--- a/solution.py
+++ b/solution.py
@@ -11,6 +11,7 @@
 DIAGONAL = 6.0 + SCREEN
 HALO = 4
 CORES = 2
+SUMS = 8
 NOISE = 1e-6
 
 
@@ -25,12 +26,12 @@
 
 def cg_kernel(
     n_band, n_gx, n_gy, owner_ref, picked_ref, local_ref, weight_ref, out_ref,
-    fields_ref, orb_ref, from_mate, combined, from_far, results, results_in,
+    fields_ref, orb_ref, orb_raw, from_mate, combined, from_far, results, results_in,
     dens, v1, v2, d2, w, coef, part, parts, send_sem, recv_sem,
     mate_sem, far_sem, orb_sem, halo_sem, result_sem,
 ):
     ex, ey, nf, nz = fields_ref.shape
-    nl = orb_ref.shape[0]
+    nl = orb_ref.shape[2]
     turns, n_chip, cores, share = picked_ref.shape[:4]
     per_band = nl // n_band
     nx, ny = ex - 2 * HALO, ey - 2 * HALO
@@ -82,14 +83,14 @@
         copy.start()
     orb_copies = [
         remote(
-            local_ref, orb_ref.at[pl.ds(band * per_band, per_band), inside_x, inside_y],
+            local_ref, orb_raw.at[pl.ds(band * per_band, per_band)],
             (orb_sem.at[0, off], orb_sem.at[1, off]), {"band": lax.rem(band + off, n_band)},
         )
         for off in range(1, n_band)
     ]
     for copy in orb_copies:
         copy.start()
-    orb_ref[pl.ds(band * per_band, per_band), inside_x, inside_y] = local_ref[...]
+    orb_raw[pl.ds(band * per_band, per_band)] = local_ref[...]
     far = []
     for t in range(turns):
         to_mate[t].wait()
@@ -107,34 +108,47 @@
             copy.start()
             far.append((t, copy))
 
-    def halo(ref, lead, which):
-        def along_x(lo, n, dst, target, k):
-            src = ref.at[lead + (pl.ds(lo, n), inside_y)]
-            dst = ref.at[lead + (pl.ds(dst, n), inside_y)]
-            return remote(src, dst, (halo_sem.at[0, which, k], halo_sem.at[1, which, k]), target)
-
-        def along_y(lo, n, dst, target, k):
-            src = ref.at[lead + (slice(None), pl.ds(lo, n))]
-            dst = ref.at[lead + (slice(None), pl.ds(dst, n))]
-            return remote(src, dst, (halo_sem.at[0, which, k], halo_sem.at[1, which, k]), target)
-
-        up, down = {"gx": lax.rem(gx + 1, n_gx)}, {"gx": lax.rem(gx + n_gx - 1, n_gx)}
-        right, left = {"gy": lax.rem(gy + 1, n_gy)}, {"gy": lax.rem(gy + n_gy - 1, n_gy)}
-        return (
-            [along_x(nx, HALO, 0, up, 0), along_x(HALO, HALO, HALO + nx, down, 1)],
-            [along_y(ny, HALO, 0, right, 2), along_y(HALO, HALO, HALO + ny, left, 3)],
-        )
+    up, down = {"gx": lax.rem(gx + 1, n_gx)}, {"gx": lax.rem(gx + n_gx - 1, n_gx)}
+    right, left = {"gy": lax.rem(gy + 1, n_gy)}, {"gy": lax.rem(gy + n_gy - 1, n_gy)}
+
+    def halo(ref, which):
+        def copy(src, dst, target, k):
+            sems = (halo_sem.at[0, which, k], halo_sem.at[1, which, k])
+            return remote(ref.at[src], ref.at[dst], sems, target)
+
+        def along_y(rows, k):
+            return [
+                copy((rows, pl.ds(ny, HALO)), (rows, pl.ds(0, HALO)), right, k),
+                copy((rows, pl.ds(HALO, HALO)), (rows, pl.ds(HALO + ny, HALO)), left, k + 1),
+            ]
+
+        along_x = [
+            copy((pl.ds(nx, HALO), inside_y), (pl.ds(0, HALO), inside_y), up, 0),
+            copy((pl.ds(HALO, HALO), inside_y), (pl.ds(HALO + nx, HALO), inside_y), down, 1),
+        ]
+        corners = [along_y(pl.ds(0, HALO), 4), along_y(pl.ds(HALO + nx, HALO), 6)]
+        return along_x, along_y(inside_x, 2), corners
+
+    def start_halo(copies):
+        for copy in copies[0] + copies[1]:
+            copy.start()
+
+    def turn_corners(copies):
+        for copy, corners in zip(copies[0], copies[2]):
+            copy.wait()
+            for corner in corners:
+                corner.start()
+
+    def finish_halo(copies):
+        for copy in copies[1] + copies[2][0] + copies[2][1]:
+            copy.wait()
 
     for copy in orb_copies:
         copy.wait()
-    orb_x, orb_y = halo(orb_ref, (slice(None),), 0)
-    field_x, field_y = halo(fields_ref, (), 1)
-    for copy in orb_x:
-        copy.start()
-    for copy in orb_x:
-        copy.wait()
-    for copy in orb_y:
-        copy.start()
+    for i in range(nl):
+        orb_ref[inside_x, inside_y, i, :] = orb_raw[i]
+    orb_halo, field_halo = halo(orb_ref, 0), halo(fields_ref, 1)
+    start_halo(orb_halo)
     for t in range(turns):
         for turn, copy in far:
             if turn == t:
@@ -146,23 +160,29 @@
             value = jnp.where(who // cores == there, from_far[off - 1, t], value)
         for s in range(share):
             fields_ref[inside_x, inside_y, t * share + s, :] = value[s]
-    for copies in (field_x, field_y):
-        for copy in copies:
-            copy.start()
-        for copy in copies:
-            copy.wait()
-    for copy in orb_y:
-        copy.wait()
-
-    def pack(sums):
-        total = jnp.zeros((nf, nz), jnp.float32)
+    turn_corners(orb_halo)
+    start_halo(field_halo)
+    turn_corners(field_halo)
+    finish_halo(orb_halo)
+    finish_halo(field_halo)
+
+    def row0(x, c):
+        f = fields_ref[x]
+        for i in range(nl):
+            dens[i, x] = f * orb_ref[x, :, i : i + 1, :]
+        return c
+
+    lax.fori_loop(0, ex, row0, 0)
+
+    def pack(r, i, sums):
+        total = part[r]
         for m, acc in enumerate(sums):
             value = jnp.sum(acc, axis=1, keepdims=True)
-            total = jnp.where(lane == m, jnp.broadcast_to(value, (nf, nz)), total)
-        return total
-
-    def unpack(total, m):
-        value = jnp.sum(jnp.where(lane == m, total, 0.0), axis=1, keepdims=True)
+            total = jnp.where(lane == i * SUMS + m, jnp.broadcast_to(value, (nf, nz)), total)
+        part[r] = total
+
+    def unpack(total, i, m):
+        value = jnp.sum(jnp.where(lane == i * SUMS + m, total, 0.0), axis=1, keepdims=True)
         return jnp.broadcast_to(value, (nf, nz))
 
     def copy_to(r, index):
@@ -195,21 +215,16 @@
         lax.fori_loop(1, group, finish, 0)
         return lax.fori_loop(1, group, lambda s, t: t + parts[r, s], parts[r, 0])
 
-    def density(i, x, lo, hi):
-        return fields_ref[x, lo:hi] * orb_ref[i, x, lo:hi]
-
     def inner(sums, pairs):
         return tuple(s + jnp.sum(a * b, axis=0) for s, (a, b) in zip(sums, pairs))
 
     zero = jnp.zeros((nf, nz), jnp.float32)
+    part[0] = zero
+    part[1] = zero
 
     def basis(i, c):
-        def row0(x, c):
-            dens[x] = density(i, x, 0, ey)
-            return c
-
         def row1(x, c):
-            v1[i, x] = apply_row(lambda p, lo, hi: dens[p, lo:hi], x + 1, ey)
+            v1[i, x] = apply_row(lambda p, lo, hi: dens[i, p, lo:hi], x + 1, ey)
             return c
 
         def row2(x, c):
@@ -217,21 +232,20 @@
             return c
 
         def products(x, sums):
-            b = dens[x + 4, 4 : 4 + ny]
+            b = dens[i, x + 4, 4 : 4 + ny]
             a1 = v1[i, x + 3, 3 : 3 + ny]
             a2 = v2[i, x + 2, 2 : 2 + ny]
             return inner(sums, ((b, b), (b, a1), (a1, a1), (a1, a2), (a2, a2)))
 
-        lax.fori_loop(0, ex, row0, 0)
         lax.fori_loop(0, ex - 2, row1, 0)
         lax.fori_loop(0, ex - 4, row2, 0)
-        part[0, i] = pack(lax.fori_loop(0, nx, products, (zero,) * 5))
+        pack(0, i, lax.fori_loop(0, nx, products, (zero,) * 5))
         return c
 
     lax.fori_loop(0, nl, basis, 0)
     total = all_reduce(0)
     for i in range(nl):
-        m0, m1, m2, m3, m4 = (unpack(total[i], m) for m in range(5))
+        m0, m1, m2, m3, m4 = (unpack(total, i, m) for m in range(5))
         s0 = m0 / m1
         rr1 = s0 * s0 * m2 - 2.0 * s0 * m1 + m0
         small = rr1 <= NOISE * m0
@@ -251,7 +265,7 @@
         c2 = s1 * s0
 
         def row_d(x, c):
-            b = density(i, x + 2, 2, ey - 2)
+            b = dens[i, x + 2, 2 : ey - 2]
             d2[i, x] = cb * b + c1 * v1[i, x + 1, 1 : ey - 3] + c2 * v2[i, x]
             return c
 
@@ -260,7 +274,7 @@
             return c
 
         def products(x, sums):
-            b = density(i, x + 4, 4, 4 + ny)
+            b = dens[i, x + 4, 4 : 4 + ny]
             a1 = v1[i, x + 3, 3 : 3 + ny]
             a2 = v2[i, x + 2, 2 : 2 + ny]
             dd = d2[i, x + 2, 2 : 2 + ny]
@@ -275,13 +289,13 @@
 
         lax.fori_loop(0, ex - 4, row_d, 0)
         lax.fori_loop(0, ex - 6, row_w, 0)
-        part[1, i] = pack(lax.fori_loop(0, nx, products, (zero,) * 7))
+        pack(1, i, lax.fori_loop(0, nx, products, (zero,) * 7))
         return c
 
     lax.fori_loop(0, nl, second, 0)
     total = all_reduce(1)
     for i in range(nl):
-        rr, rw, dw, ww, ra, wa, waw = (unpack(total[i], m) for m in range(7))
+        rr, rw, dw, ww, ra, wa, waw = (unpack(total, i, m) for m in range(7))
         b1 = coef[i, 3]
         s2 = rr / dw
         rr3 = rr - 2.0 * s2 * rw + s2 * s2 * ww
@@ -306,7 +320,7 @@
 
         def row(x, c):
             f = fields_ref[x + 4, 4 : 4 + ny]
-            b = f * orb_ref[i, x + 4, 4 : 4 + ny]
+            b = dens[i, x + 4, 4 : 4 + ny]
             sol = cb * b + c1 * v1[i, x + 3, 3 : 3 + ny]
             sol = sol + cd * d2[i, x + 2, 2 : 2 + ny] + cw * w[i, x + 1, 1 : 1 + ny]
             results[i, x] = -jnp.sum(sol * f, axis=1)
@@ -354,26 +368,27 @@
         out_specs=vmem,
         scratch_shapes=[
             pltpu.VMEM((ex, ey, nf, nz), f32),
-            pltpu.VMEM((nl, ex, ey, 1, nz), f32),
+            pltpu.VMEM((ex, ey, nl, nz), f32),
+            pltpu.VMEM((nl, nx, ny, nz), f32),
             pltpu.VMEM((turns, n_chip, share, nx, ny, nz), f32),
             pltpu.VMEM((n_chip - 1, turns, share, nx, ny, nz), f32),
             pltpu.VMEM((n_chip - 1, turns, share, nx, ny, nz), f32),
             pltpu.VMEM((nl, nx, ny, nz), f32),
             pltpu.VMEM((n_band - 1, per_band, nx, ny, nz), f32),
-            pltpu.VMEM((ex, ey, nf, nz), f32),
+            pltpu.VMEM((nl, ex, ey, nf, nz), f32),
             pltpu.VMEM((nl, ex - 2, ey - 2, nf, nz), f32),
             pltpu.VMEM((nl, ex - 4, ey - 4, nf, nz), f32),
             pltpu.VMEM((nl, ex - 4, ey - 4, nf, nz), f32),
             pltpu.VMEM((nl, ex - 6, ey - 6, nf, nz), f32),
             pltpu.VMEM((nl, 7, nf, nz), f32),
-            pltpu.VMEM((2, nl, nf, nz), f32),
-            pltpu.VMEM((2, group, nl, nf, nz), f32),
+            pltpu.VMEM((2, nf, nz), f32),
+            pltpu.VMEM((2, group, nf, nz), f32),
             pltpu.SemaphoreType.DMA((2, group)),
             pltpu.SemaphoreType.DMA((2, group)),
             pltpu.SemaphoreType.DMA((2, turns)),
             pltpu.SemaphoreType.DMA((2, n_chip - 1, turns)),
             pltpu.SemaphoreType.DMA((2, n_band)),
-            pltpu.SemaphoreType.DMA((2, 2, 4)),
+            pltpu.SemaphoreType.DMA((2, 2, 8)),
             pltpu.SemaphoreType.DMA((2, n_band - 1)),
         ],
         compiler_params=pltpu.CompilerParams(
@@ -393,7 +408,7 @@
     weights = occupation[owner * blocks_dev + block_id]
     weights = lax.dynamic_slice_in_dim(weights, band * share, share, axis=1)
     weight = jnp.broadcast_to(weights.reshape(-1, 1), (turns * share, nz))
-    return run(mesh, owner, picked, local_orbitals[:, :, :, None, :], weight)
+    return run(mesh, owner, picked, local_orbitals, weight)
 
 
 def solution(mesh):

time: 90.8 us -> 80.8 us (0.89)
  Pallas kernels: 83.8 us -> 73.9 us
    pallas_call x1, Pallas kernels: 83.8 us -> 73.9 us  [run(): pl.pallas_call(functools.partial(cg_kernel, n_band, n_gx, n_gy), out_shap...]
where the time goes in v3:
time: 80.8 us; the launch traced here: 80.7 us
  Pallas kernels  73.9 us (91%)
  local copies, waits for them, and re-layouts  5.95 us (7%)
  other arithmetic  0.83 us (1%)
    pallas_call x1, Pallas kernels, run(): pl.pallas_call(functools.partial(cg_kernel, n_band, n_gx, n_gy), out_shap...  73.9 us
    unnamed x10, local copies, waits for them, and re-layouts  3.13 us
    gather x1, local copies, waits for them, and re-layouts, on_device(): picked = block_orbitals[block_id]  2.02 us

profile of v3, /device:TPU:0, one launch (start us, length us, event | category | flops | bytes accessed | tf_op | source)
XLA Modules:
  0.0 80.7 jit_solution(18358204877270833291)
XLA Ops:
  0.0 0.0 copy-start
  0.0 0.8 %compare_select_fusion = (s32[4]{0:T(128)S(1)}, s32[4]{0:T(128)S(1)}) fusion(s32[4]{0:T(128)} %param.9, s32[4]{0:T(128)} %owner_ref.1), kind=kLoop, calls=%fused_computation.4 | loop fusion | flops 32 | bytes 64 | tf_op jit(solution)/shard_map/select_n | solution.py:408
  0.8 0.9 %copy.7 = f32[24,8]{1,0:T(8,128)S(1)} copy(f32[24,8]{0,1:T(8,128)} %param.7) | data formatting | bytes 1536 | tf_op args[2]
  1.7 0.6 gather_fusion.1
  2.3 0.1 constant_dynamic-slice_fusion
  2.4 0.1 broadcast_in_dim.15
  2.5 0.1 broadcast_in_dim.16.weight_ref
  2.5 0.0 copy-done
  2.5 0.0 copy-start.2
  2.5 0.0 copy-start.3
  2.5 2.0 %gather_fusion = f32[4,8,8,16,128]{4,3,2,1,0:T(8,128)} fusion(f32[6,8,8,16,128]{4,3,2,1,0:T(8,128)S(1)} %copy-done, s32[1024]{0:T(1024)S(1)} %get-tuple-element.8), kind=kCustom, calls=%fused_computation | custom fusion | bytes 4194320 | tf_op jit(solution)/shard_map/gather | solution.py:406
  4.6 0.0 copy-done.2
  4.6 0.0 copy-done.3
  4.6 0.0 copy-start.1
  4.6 1.6 %copy-done.1 = f32[4,8,8,16,128]{4,3,2,1,0:T(8,128)S(1)} copy-done((f32[4,8,8,16,128]{4,3,2,1,0:T(8,128)S(1)}, f32[4,8,8,16,128]{4,3,2,1,0:T(8,128)}, u32[]{:S(2)}) %copy-start.1) | copy-done | bytes 2097176
  6.2 73.9 %shard_map.55 = f32[1,8,16,128]{3,2,1,0:T(8,128)S(1)} custom-call(s32[4]{0:T(128)S(1)} %copy-done.3, f32[4,2,2,2,8,16,128]{6,5,4,3,2,1,0:T(8,128)S(1)} %bitcast.1, f32[1,8,16,128]{3,2,1,0:T(8,128)S(1)} %copy-done.2, f32[8,128]{1,0:T(8,128)S(1)} %broadcast_in_dim.16.weight_ref), custom_call_target="tpu_custom_call" | custom-call | tf_op jit(solution)/shard_map/pallas_call | solution.py:364
  80.0 0.6 copy.9
  (1 shorter events, 0.0 us)
Async XLA Ops:
  0.0 2.5 %copy-start = (f32[6,8,8,16,128]{4,3,2,1,0:T(8,128)S(1)}, f32[6,8,8,16,128]{4,3,2,1,0:T(8,128)}, u32[]{:S(2)}) copy-start(f32[6,8,8,16,128]{4,3,2,1,0:T(8,128)} %param.6) | copy-start | bytes 9437188
  2.5 2.0 %copy-start.2 = (f32[1,8,16,128]{3,2,1,0:T(8,128)S(1)}, f32[1,8,16,128]{3,2,1,0:T(8,128)}, u32[]{:S(2)}) copy-start(f32[1,8,16,128]{3,2,1,0:T(8,128)} %local_ref.1) | copy-start | bytes 196612
  2.5 2.0 %copy-start.3 = (s32[4]{0:T(128)S(1)}, s32[4]{0:T(128)}, u32[]{:S(2)}) copy-start(s32[4]{0:T(128)} %owner_ref.1) | copy-start | bytes 52
  4.6 1.6 %copy-start.1 = (f32[4,8,8,16,128]{4,3,2,1,0:T(8,128)S(1)}, f32[4,8,8,16,128]{4,3,2,1,0:T(8,128)}, u32[]{:S(2)}) copy-start(f32[4,8,8,16,128]{4,3,2,1,0:T(8,128)} %gather_fusion) | copy-start | bytes 6291460

commit v4 on v3

--- a/solution.py
+++ b/solution.py
@@ -26,9 +26,9 @@
 
 def cg_kernel(
     n_band, n_gx, n_gy, owner_ref, picked_ref, local_ref, weight_ref, out_ref,
-    fields_ref, orb_ref, orb_raw, from_mate, combined, from_far, results, results_in,
+    fields_ref, orb_ref, orb_raw, arrived, beside, from_mate, combined, from_far, results, results_in,
     dens, v1, v2, d2, w, coef, part, parts, send_sem, recv_sem,
-    mate_sem, far_sem, orb_sem, halo_sem, result_sem,
+    mate_sem, far_sem, orb_sem, halo_sem, result_sem, beside_sem,
 ):
     ex, ey, nf, nz = fields_ref.shape
     nl = orb_ref.shape[2]
@@ -149,6 +149,7 @@
         orb_ref[inside_x, inside_y, i, :] = orb_raw[i]
     orb_halo, field_halo = halo(orb_ref, 0), halo(fields_ref, 1)
     start_halo(orb_halo)
+    rows_in = []
     for t in range(turns):
         for turn, copy in far:
             if turn == t:
@@ -158,11 +159,27 @@
         for off in range(1, n_chip):
             there = lax.rem(chip + n_chip - off, n_chip)
             value = jnp.where(who // cores == there, from_far[off - 1, t], value)
+        arrived[t] = value
+        for k, (first, target) in enumerate(((nx - HALO, up), (0, down))):
+            copy = remote(
+                arrived.at[t, :, pl.ds(first, HALO)], beside.at[k, t],
+                (beside_sem.at[0, k, t], beside_sem.at[1, k, t]), target,
+            )
+            copy.start()
+            rows_in.append((k, t, copy))
         for s in range(share):
             fields_ref[inside_x, inside_y, t * share + s, :] = value[s]
     turn_corners(orb_halo)
-    start_halo(field_halo)
-    turn_corners(field_halo)
+    for copy in field_halo[1]:
+        copy.start()
+    for k, t, copy in rows_in:
+        copy.wait()
+        for s in range(share):
+            rows = pl.ds(k * (HALO + nx), HALO)
+            fields_ref[rows, inside_y, t * share + s, :] = beside[k, t, s]
+    for corners in field_halo[2]:
+        for corner in corners:
+            corner.start()
     finish_halo(orb_halo)
     finish_halo(field_halo)
 
@@ -370,6 +387,8 @@
             pltpu.VMEM((ex, ey, nf, nz), f32),
             pltpu.VMEM((ex, ey, nl, nz), f32),
             pltpu.VMEM((nl, nx, ny, nz), f32),
+            pltpu.VMEM((turns, share, nx, ny, nz), f32),
+            pltpu.VMEM((2, turns, share, HALO, ny, nz), f32),
             pltpu.VMEM((turns, n_chip, share, nx, ny, nz), f32),
             pltpu.VMEM((n_chip - 1, turns, share, nx, ny, nz), f32),
             pltpu.VMEM((n_chip - 1, turns, share, nx, ny, nz), f32),
@@ -390,6 +409,7 @@
             pltpu.SemaphoreType.DMA((2, n_band)),
             pltpu.SemaphoreType.DMA((2, 2, 8)),
             pltpu.SemaphoreType.DMA((2, n_band - 1)),
+            pltpu.SemaphoreType.DMA((2, 2, turns)),
         ],
         compiler_params=pltpu.CompilerParams(
             collective_id=0, has_side_effects=True, vmem_limit_bytes=50 << 20

time: 80.8 us -> 80.3 us (level)
  no operation moved by 1% of the time
where the time goes in v4:
time: 80.3 us; the launch traced here: 80 us
  Pallas kernels  73.2 us (91%)
  local copies, waits for them, and re-layouts  5.95 us (7%)
  other arithmetic  0.83 us (1%)
    pallas_call x1, Pallas kernels, run(): pl.pallas_call(functools.partial(cg_kernel, n_band, n_gx, n_gy), out_shap...  73.2 us
    unnamed x10, local copies, waits for them, and re-layouts  3.13 us
    gather x1, local copies, waits for them, and re-layouts, on_device(): picked = block_orbitals[block_id]  2.02 us

profile of v4, /device:TPU:0, one launch (start us, length us, event | category | flops | bytes accessed | tf_op | source)
XLA Modules:
  0.0 80.0 jit_solution(1720888623208435873)
XLA Ops:
  0.0 0.0 copy-start
  0.0 0.8 %compare_select_fusion = (s32[4]{0:T(128)S(1)}, s32[4]{0:T(128)S(1)}) fusion(s32[4]{0:T(128)} %param.9, s32[4]{0:T(128)} %owner_ref.1), kind=kLoop, calls=%fused_computation.4 | loop fusion | flops 32 | bytes 64 | tf_op jit(solution)/shard_map/select_n | solution.py:428
  0.8 0.9 %copy.7 = f32[24,8]{1,0:T(8,128)S(1)} copy(f32[24,8]{0,1:T(8,128)} %param.7) | data formatting | bytes 1536 | tf_op args[2]
  1.7 0.6 gather_fusion.1
  2.3 0.1 constant_dynamic-slice_fusion
  2.4 0.1 broadcast_in_dim.15
  2.5 0.1 broadcast_in_dim.16.weight_ref
  2.5 0.0 copy-done
  2.5 0.0 copy-start.2
  2.5 0.0 copy-start.3
  2.5 2.0 %gather_fusion = f32[4,8,8,16,128]{4,3,2,1,0:T(8,128)} fusion(f32[6,8,8,16,128]{4,3,2,1,0:T(8,128)S(1)} %copy-done, s32[1024]{0:T(1024)S(1)} %get-tuple-element.8), kind=kCustom, calls=%fused_computation | custom fusion | bytes 4194320 | tf_op jit(solution)/shard_map/gather | solution.py:426
  4.6 0.0 copy-done.2
  4.6 0.0 copy-done.3
  4.6 0.0 copy-start.1
  4.6 1.6 %copy-done.1 = f32[4,8,8,16,128]{4,3,2,1,0:T(8,128)S(1)} copy-done((f32[4,8,8,16,128]{4,3,2,1,0:T(8,128)S(1)}, f32[4,8,8,16,128]{4,3,2,1,0:T(8,128)}, u32[]{:S(2)}) %copy-start.1) | copy-done | bytes 2097176
  6.2 73.2 %shard_map.55 = f32[1,8,16,128]{3,2,1,0:T(8,128)S(1)} custom-call(s32[4]{0:T(128)S(1)} %copy-done.3, f32[4,2,2,2,8,16,128]{6,5,4,3,2,1,0:T(8,128)S(1)} %bitcast.1, f32[1,8,16,128]{3,2,1,0:T(8,128)S(1)} %copy-done.2, f32[8,128]{1,0:T(8,128)S(1)} %broadcast_in_dim.16.weight_ref), custom_call_target="tpu_custom_call" | custom-call | tf_op jit(solution)/shard_map/pallas_call | solution.py:381
  79.4 0.6 copy.9
  (1 shorter events, 0.0 us)
Async XLA Ops:
  0.0 2.5 %copy-start = (f32[6,8,8,16,128]{4,3,2,1,0:T(8,128)S(1)}, f32[6,8,8,16,128]{4,3,2,1,0:T(8,128)}, u32[]{:S(2)}) copy-start(f32[6,8,8,16,128]{4,3,2,1,0:T(8,128)} %param.6) | copy-start | bytes 9437188
  2.5 2.0 %copy-start.2 = (f32[1,8,16,128]{3,2,1,0:T(8,128)S(1)}, f32[1,8,16,128]{3,2,1,0:T(8,128)}, u32[]{:S(2)}) copy-start(f32[1,8,16,128]{3,2,1,0:T(8,128)} %local_ref.1) | copy-start | bytes 196612
  2.5 2.0 %copy-start.3 = (s32[4]{0:T(128)S(1)}, s32[4]{0:T(128)}, u32[]{:S(2)}) copy-start(s32[4]{0:T(128)} %owner_ref.1) | copy-start | bytes 52
  4.6 1.6 %copy-start.1 = (f32[4,8,8,16,128]{4,3,2,1,0:T(8,128)S(1)}, f32[4,8,8,16,128]{4,3,2,1,0:T(8,128)}, u32[]{:S(2)}) copy-start(f32[4,8,8,16,128]{4,3,2,1,0:T(8,128)} %gather_fusion) | copy-start | bytes 6291460

commit v5 on v4

--- a/solution.py
+++ b/solution.py
@@ -423,9 +423,9 @@
     turns = owner.shape[0]
     blocks_dev, block, nx, ny, nz = block_orbitals.shape
     share = block // n_band
-    picked = block_orbitals[block_id]
+    picked = block_orbitals.at[block_id].get(mode="promise_in_bounds")
     picked = picked.reshape(turns, n_band // CORES, CORES, share, nx, ny, nz)
-    weights = occupation[owner * blocks_dev + block_id]
+    weights = occupation.at[owner * blocks_dev + block_id].get(mode="promise_in_bounds")
     weights = lax.dynamic_slice_in_dim(weights, band * share, share, axis=1)
     weight = jnp.broadcast_to(weights.reshape(-1, 1), (turns * share, nz))
     return run(mesh, owner, picked, local_orbitals, weight)

time: 80.3 us -> 80.3 us (level)
  no operation moved by 1% of the time
where the time goes in v5:
time: 80.3 us; the launch traced here: 80 us
  Pallas kernels  73.2 us (91%)
  local copies, waits for them, and re-layouts  5.95 us (7%)
  other arithmetic  0.83 us (1%)
    pallas_call x1, Pallas kernels, run(): pl.pallas_call(functools.partial(cg_kernel, n_band, n_gx, n_gy), out_shap...  73.2 us
    unnamed x10, local copies, waits for them, and re-layouts  3.13 us
    gather x1, local copies, waits for them, and re-layouts, on_device(): picked = block_orbitals.at[block_id].get(mode='promise_in_bounds')  2.02 us

profile of v5, /device:TPU:0, one launch (start us, length us, event | category | flops | bytes accessed | tf_op | source)
XLA Modules:
  0.0 80.0 jit_solution(1720888623208435873)
XLA Ops:
  0.0 0.0 copy-start
  0.0 0.8 %compare_select_fusion = (s32[4]{0:T(128)S(1)}, s32[4]{0:T(128)S(1)}) fusion(s32[4]{0:T(128)} %param.9, s32[4]{0:T(128)} %owner_ref.1), kind=kLoop, calls=%fused_computation.4 | loop fusion | flops 32 | bytes 64 | tf_op jit(solution)/shard_map/select_n | solution.py:428
  0.8 0.9 %copy.7 = f32[24,8]{1,0:T(8,128)S(1)} copy(f32[24,8]{0,1:T(8,128)} %param.7) | data formatting | bytes 1536 | tf_op args[2]
  1.7 0.6 gather_fusion.1
  2.3 0.1 constant_dynamic-slice_fusion
  2.4 0.1 broadcast_in_dim.15
  2.5 0.1 broadcast_in_dim.16.weight_ref
  2.5 0.0 copy-done
  2.5 0.0 copy-start.2
  2.5 0.0 copy-start.3
  2.5 2.0 %gather_fusion = f32[4,8,8,16,128]{4,3,2,1,0:T(8,128)} fusion(f32[6,8,8,16,128]{4,3,2,1,0:T(8,128)S(1)} %copy-done, s32[1024]{0:T(1024)S(1)} %get-tuple-element.8), kind=kCustom, calls=%fused_computation | custom fusion | bytes 4194320 | tf_op jit(solution)/shard_map/gather | solution.py:426
  4.6 0.0 copy-done.2
  4.6 0.0 copy-done.3
  4.6 0.0 copy-start.1
  4.6 1.6 %copy-done.1 = f32[4,8,8,16,128]{4,3,2,1,0:T(8,128)S(1)} copy-done((f32[4,8,8,16,128]{4,3,2,1,0:T(8,128)S(1)}, f32[4,8,8,16,128]{4,3,2,1,0:T(8,128)}, u32[]{:S(2)}) %copy-start.1) | copy-done | bytes 2097176
  6.2 73.2 %shard_map.55 = f32[1,8,16,128]{3,2,1,0:T(8,128)S(1)} custom-call(s32[4]{0:T(128)S(1)} %copy-done.3, f32[4,2,2,2,8,16,128]{6,5,4,3,2,1,0:T(8,128)S(1)} %bitcast.1, f32[1,8,16,128]{3,2,1,0:T(8,128)S(1)} %copy-done.2, f32[8,128]{1,0:T(8,128)S(1)} %broadcast_in_dim.16.weight_ref), custom_call_target="tpu_custom_call" | custom-call | tf_op jit(solution)/shard_map/pallas_call | solution.py:381
  79.4 0.6 copy.9
  (1 shorter events, 0.0 us)
Async XLA Ops:
  0.0 2.5 %copy-start = (f32[6,8,8,16,128]{4,3,2,1,0:T(8,128)S(1)}, f32[6,8,8,16,128]{4,3,2,1,0:T(8,128)}, u32[]{:S(2)}) copy-start(f32[6,8,8,16,128]{4,3,2,1,0:T(8,128)} %param.6) | copy-start | bytes 9437188
  2.5 2.0 %copy-start.2 = (f32[1,8,16,128]{3,2,1,0:T(8,128)S(1)}, f32[1,8,16,128]{3,2,1,0:T(8,128)}, u32[]{:S(2)}) copy-start(f32[1,8,16,128]{3,2,1,0:T(8,128)} %local_ref.1) | copy-start | bytes 196612
  2.5 2.0 %copy-start.3 = (s32[4]{0:T(128)S(1)}, s32[4]{0:T(128)}, u32[]{:S(2)}) copy-start(s32[4]{0:T(128)} %owner_ref.1) | copy-start | bytes 52
  4.6 1.6 %copy-start.1 = (f32[4,8,8,16,128]{4,3,2,1,0:T(8,128)S(1)}, f32[4,8,8,16,128]{4,3,2,1,0:T(8,128)}, u32[]{:S(2)}) copy-start(f32[4,8,8,16,128]{4,3,2,1,0:T(8,128)} %gather_fusion) | copy-start | bytes 6291460
